TPU v7x, 512 devices: a whole 4x8x8 slice. The times are simulated.
512 devices in a mesh: row: 32 (over z, y_hi), col: 16 (over y_lo, x, core).
Axes of the slice: x: 4, y: 8 (y_hi: 4, y_lo: 2; y = y_hi * 2 + y_lo), z: 8, core: 2. Of those that a mesh axis runs over, the one named last changes fastest.
Arguments:
- inverse_block: bfloat16 [20480, 20480], P('row', 'col')
- factor_cols: bfloat16 [3, 20480, 512], P(None, 'col', 'row'), may hold values from -6 to 6
- occupancy: int32 [3, 160], replicated, may hold values 0 or 1
- row_block: int32 [3, 160], replicated, may hold values from 0 to 159, each once within a row
- coupling: bfloat16 [2, 512, 512], replicated, may hold values from -0.25 to 0.25
- diag_inverse: float32 [3, 512, 512], P(None, None, 'col'), may hold values from -6 to 6
Outputs:
- columns: float32 [3, 20480, 512], P(None, ('row', 'col'))
- diagonals: float32 [3, 512, 512], P(None, None, 'col')
Inputs may be any that keep to these rules, and one draw needn't show every extreme that they name: `row_block`: each row names every one of the 160 row blocks exactly once.
All inputs are finite; a program needn't handle non-finite values.
Results may differ from a plain program's by a relative error of at most 0.0003.
Values may be sent and summed in bfloat16 or wider, within the bound.
A program may use at most 64 MiB of HBM per device.

v0:
```python
import jax
import jax.numpy as jnp
from jax import lax
from jax.sharding import PartitionSpec as P

highest = lax.Precision.HIGHEST


def routed(gathered, occupancy, row_block, nblocks):
    count = gathered.shape[0]
    width_part = gathered.shape[1] // (nblocks * 128)
    blocks = gathered.reshape(count, nblocks, 128, width_part)
    levels = lax.broadcasted_iota(jnp.int32, (count, nblocks, nblocks), 1)
    picks = ((row_block[:, None, :] == levels) & (occupancy[:, None, :] > 0)).astype(jnp.bfloat16)
    placed = jnp.einsum("kqb,kbtx->kxqt", picks, blocks, preferred_element_type=jnp.float32)
    return placed.astype(jnp.bfloat16).reshape(count, width_part, nblocks * 128)


def split_rows(placed, column, row_parts, col_parts, tile):
    count, width_part, total = placed.shape
    span = total // col_parts
    column_part = lax.dynamic_slice_in_dim(placed, column * span, span, 2)
    grid = placed.reshape(count, width_part, row_parts, col_parts, tile)
    mine = lax.dynamic_index_in_dim(grid, column, 3, keepdims=False)
    return (column_part, jnp.transpose(mine, (0, 2, 1, 3)))


def make_term(inverse_block, column_full):
    return lax.dot_general(
        inverse_block, column_full, (((1,), (2,)), ((), ())), preferred_element_type=jnp.float32
    )


def local_step(summed, own_rows, previous, link, diag_part, column, row_first, rows_total):
    if link is None:
        coupled = jnp.zeros_like(summed)
    else:
        coupled = jnp.dot(previous, link.astype(jnp.float32), precision=highest)
    current = -(summed + coupled)
    own = own_rows.astype(jnp.float32)
    inner = jnp.dot(own, current, precision=highest) - jnp.dot(coupled.T, own.T, precision=highest)
    width = summed.shape[1]
    diag_cols = diag_part.shape[1]
    embedded = lax.dynamic_update_slice(
        jnp.zeros((width, width), jnp.float32), diag_part, (0, column * diag_cols)
    )
    return (current, row_first * embedded - inner / rows_total)


def chain_diag(total, chain_prev, link):
    if link is None:
        return total
    link_wide = link.astype(jnp.float32)
    return total + jnp.dot(
        link_wide.T, jnp.dot(chain_prev, link_wide, precision=highest), precision=highest
    )


def per_device(inverse_block, factor_cols, occupancy, row_block, coupling, diag_inverse):
    column = lax.axis_index("col")
    row_first = (lax.axis_index("row") == 0).astype(jnp.float32)
    row_parts = lax.axis_size("row")
    col_parts = lax.axis_size("col")
    local_rows = inverse_block.shape[0]
    rows_total = local_rows * row_parts
    supers, span, width_part = factor_cols.shape
    width = width_part * row_parts
    tile = local_rows // col_parts
    nblocks = occupancy.shape[1]
    diag_cols = diag_inverse.shape[2]
    flat = factor_cols.reshape(supers, span * width_part)
    column_list = []
    partial_list = []
    previous = None
    for position in range(supers):
        gathered = lax.all_gather(flat[position : position + 1], "col", axis=1, tiled=True)
        placed = routed(
            gathered,
            occupancy[position : position + 1],
            row_block[position : position + 1],
            nblocks,
        )
        column_part, outgoing = split_rows(placed, column, row_parts, col_parts, tile)
        column_full = lax.all_gather(column_part, "row", axis=1, tiled=True)
        arrived = lax.all_to_all(outgoing, "row", split_axis=1, concat_axis=1, tiled=True)
        summed = lax.psum_scatter(
            make_term(inverse_block, column_full), "col", scatter_dimension=0, tiled=True
        )
        link = None if position == 0 else coupling[position - 1]
        current, partial_value = local_step(
            summed[:, 0, :],
            arrived.reshape(width, tile),
            previous,
            link,
            diag_inverse[position],
            column,
            row_first,
            rows_total,
        )
        column_list.append(current)
        partial_list.append(partial_value)
        previous = current
    diag_list = []
    totals = lax.psum(jnp.stack(partial_list), ("row", "col"))
    chain_prev = None
    for position in range(supers):
        link = None if position == 0 else coupling[position - 1]
        diag_now = chain_diag(totals[position], chain_prev, link)
        diag_list.append(lax.dynamic_slice_in_dim(diag_now, column * diag_cols, diag_cols, 1))
        chain_prev = diag_now
    diagonals = jnp.stack(diag_list)
    return (jnp.stack(column_list), diagonals)


def solution(mesh):
    in_specs = (P("row", "col"), P(None, "col", "row"), P(), P(), P(), P(None, None, "col"))
    out_specs = (P(None, ("row", "col"), None), P(None, None, "col"))
    return jax.shard_map(
        per_device, mesh=mesh, in_specs=in_specs, out_specs=out_specs, check_vma=False
    )
```

profile of v0, /device:TPU:6, one launch (start us, length us, event | category | flops | bytes accessed | tf_op | source)
XLA Modules:
  0.0 764.3 jit_solution(6525715898854247528)
XLA Ops:
  7.2 0.9 fusion.67
  8.6 22.7 %all_gather.20 = bf16[1,327680]{1,0:T(2,128)(2,1)S(1)} all-gather(bf16[1,20480]{1,0:T(2,128)(2,1)S(1)} %slice.69), channel_id=1, replica_groups=mesh['row'=32,'col'=16] {'col'}, dimensions={1}, use_global_device_ids=true | all-gather | bytes 696320 | tf_op jit(solution)/shard_map/all_gather | solution.py:76
  31.3 14.5 %reduce.3 = bf16[327680]{0:T(1024)(128)(2,1)} reduce(bf16[1,327680]{1,0:T(2,128)(2,1)S(1)} %all_gather.20, bf16[]{:T(256)} %constant.52), dimensions={0}, to_apply=%all_gather.20.reduce_sub_computation | reduce | bytes 1310722 | tf_op jit(solution)/shard_map/all_gather | solution.py:76
  45.8 6.4 reshape.188
  52.3 4.0 copy.64
  58.1 22.7 %all_gather.22 = bf16[1,327680]{1,0:T(2,128)(2,1)} all-gather(bf16[1,20480]{1,0:T(2,128)(2,1)S(1)} %slice.74), channel_id=1, replica_groups=mesh['row'=32,'col'=16] {'col'}, dimensions={1}, use_global_device_ids=true | all-gather | bytes 696320 | tf_op jit(solution)/shard_map/all_gather | solution.py:76
  80.8 14.6 %reduce.5 = bf16[327680]{0:T(1024)(128)(2,1)S(1)} reduce(bf16[1,327680]{1,0:T(2,128)(2,1)} %all_gather.22, bf16[]{:T(256)} %constant.52), dimensions={0}, to_apply=%all_gather.22.reduce_sub_computation | reduce | bytes 1310722 | tf_op jit(solution)/shard_map/all_gather | solution.py:76
  95.4 4.9 reshape.191
  100.4 4.9 copy.67
  105.2 1.4 fusion.15
  106.7 1.1 reshape.192
  107.8 1.4 constant_dynamic-slice_fusion.5
  109.7 28.0 %all_gather.18 = bf16[1,327680]{1,0:T(2,128)(2,1)} all-gather(bf16[1,20480]{1,0:T(2,128)(2,1)S(1)} %slice.65), channel_id=1, replica_groups=mesh['row'=32,'col'=16] {'col'}, dimensions={1}, use_global_device_ids=true | all-gather | bytes 696320 | tf_op jit(solution)/shard_map/all_gather | solution.py:76
  137.8 15.5 %reduce.1 = bf16[327680]{0:T(1024)(128)(2,1)} reduce(bf16[1,327680]{1,0:T(2,128)(2,1)} %all_gather.18, bf16[]{:T(256)} %constant.52), dimensions={0}, to_apply=%all_gather.18.reduce_sub_computation | reduce | bytes 1310722 | tf_op jit(solution)/shard_map/all_gather | solution.py:76
  153.2 6.5 reshape.185
  159.8 4.9 copy.61
  164.7 2.3 fusion.13
  166.9 2.2 reshape.186
  169.1 1.4 constant_dynamic-slice_fusion.7
  170.6 3.6 convolution_bitcast_fusion.1
  174.2 3.8 copy.65
  178.1 49.1 %all-gather.8.cloned.1.call-done = bf16[1,512,1280]{2,1,0:T(8,128)(2,1)} async-done(((bf16[1,16,1280]{2,1,0:T(8,128)(2,1)}), bf16[1,512,1280]{2,1,0:T(8,128)(2,1)}) %all-gather.8.cloned.1.call-update) | async-done | bytes 1310736 | tf_op jit(solution)/shard_map/all_gather | solution.py:84
  227.2 3.6 convolution_bitcast_fusion
  230.7 3.8 copy.68
  234.5 76.1 %all-gather.4.cloned.1.call-done = bf16[1,512,1280]{2,1,0:T(8,128)(2,1)} async-done(((bf16[1,16,1280]{2,1,0:T(8,128)(2,1)}), bf16[1,512,1280]{2,1,0:T(8,128)(2,1)}) %all-gather.4.cloned.1.call-update) | async-done | bytes 1310736 | tf_op jit(solution)/shard_map/all_gather | solution.py:84
  310.7 3.6 convolution_bitcast_fusion.2
  314.3 3.9 copy.62
  318.2 4.1 reshape_reshape.10
  322.3 4.1 reshape_reshape.11
  326.4 2.3 constant_dynamic-slice_fusion.2
  328.9 0.8 reshape.211
  329.7 6.6 all-to-all-start.1
  336.4 4.1 reshape_reshape.9
  340.6 0.8 reshape.209
  341.5 7.1 all-to-all-done.1
  348.6 5.0 all-to-all-start.2
  353.7 1.5 constant_dynamic-slice_fusion.4
  355.4 0.8 reshape.213
  356.2 9.7 %all-to-all-done.2 = bf16[32,2,320]{2,1,0:T(2,128)(2,1)S(1)} async-done(((bf16[32,2,320]{2,1,0:T(2,128)(2,1)}), bf16[32,2,320]{2,1,0:T(2,128)(2,1)S(1)}, u32[]{:S(2)}, u32[]{:S(2)}) %all-to-all-start.2) | async-done | bytes 40992 | tf_op jit(solution)/shard_map/all_to_all | solution.py:85
  365.9 3.9 all-to-all-start
  370.3 1.3 dynamic-slice.1
  372.3 2.3 dynamic_update_slice.10
  374.8 2.3 dynamic_update_slice.11
  377.1 1.1 copy-done.9
  378.3 2.3 dynamic_update_slice.9
  380.9 1.1 all-to-all-done
  382.7 69.0 %all-reduce.9.cloned.1.call-done = (f32[640,1,512]{2,1,0:T(1,128)}, f32[640,1,512]{2,1,0:T(1,128)}, f32[640,1,512]{2,1,0:T(1,128)}) async-done(((f32[640,1,512]{2,1,0:T(1,128)}, f32[640,1,512]{2,1,0:T(1,128)}, f32[640,1,512]{2,1,0:T(1,128)}), (f32[640,1,512]{2,1,0:T(1,128)}, f32[640,1,512]{2,1,0:T(1,128)}, f32[640,1,512]{2,1,0:T(1,128)})) %all-reduce.9.cloned.1.call-update) | async-done | bytes 3932176
  451.8 1.0 dynamic-slice_negate_fusion
  452.7 0.9 constant_dynamic-slice_fusion.9
  454.9 0.9 constant_dynamic-slice_fusion.8
  455.8 0.7 fusion.5
  457.1 0.6 copy-done.10
  457.8 0.7 fusion.8
  459.0 0.7 fusion.2
  459.7 2.0 pad_maximum_fusion
  461.7 1.0 fusion.89
  462.8 0.7 pad_maximum_fusion.1
  463.5 285.1 %all-reduce.7.cloned.1.call-done = f32[3,512,512]{2,1,0:T(8,128)} async-done(((f32[3,512,512]{2,1,0:T(8,128)}), f32[3,512,512]{2,1,0:T(8,128)}) %all-reduce.7.cloned.1.call-update) | async-done | bytes 3145744 | tf_op jit(solution)/shard_map/psum | solution.py:104
  748.6 2.2 fusion.16
  750.8 2.3 fusion.9
  753.1 1.0 fusion.19
  754.2 1.1 convolution_bitcast_fusion.3
  755.3 0.7 copy-done.4
  756.8 0.7 pad_maximum_fusion.2
  (74 shorter events, 8.6 us)
Async XLA Ops:
  7.2 163.5 %copy-start = (bf16[640,1280]{1,0:T(8,128)(2,1)S(1)}, bf16[640,1280]{1,0:T(8,128)(2,1)}, u32[]{:S(2)}) copy-start(bf16[640,1280]{1,0:T(8,128)(2,1)} %param.6) | copy-start | bytes 4915204
  7.2 163.4 %all-gather.6.cloned.1.call-start = ((), (), s32[]{:S(2)}) async-start(), calls=%async_computation.4 | async-start | bytes 1351680 | tf_op jit(solution)/shard_map/all_gather | solution.py:84
  52.3 4.0 copy-start.12
  52.3 4.0 copy-start.13
  57.6 169.5 %all-gather.8.cloned.1.call-start = ((), (), s32[]{:S(2)}) async-start(), calls=%async_computation.5 | async-start | bytes 1351680 | tf_op jit(solution)/shard_map/all_gather | solution.py:84
  109.2 201.5 %all-gather.4.cloned.1.call-start = ((), (), s32[]{:S(2)}) async-start(), calls=%async_computation.3 | async-start | bytes 1351680 | tf_op jit(solution)/shard_map/all_gather | solution.py:84
  170.6 281.2 %all-reduce.9.cloned.1.call-start = ((), (), s32[]{:S(2)}) async-start(), calls=%async_computation.7 | async-start | bytes 7864320
  326.4 9.9 %copy-start.3 = (bf16[1,16,160,128]{3,2,1,0:T(8,128)(2,1)S(1)}, bf16[1,16,160,128]{3,2,1,0:T(8,128)(2,1)}, u32[]{:S(2)}) copy-start(bf16[1,16,160,128]{3,2,1,0:T(8,128)(2,1)} %fusion.13) | copy-start | bytes 1966084
  329.7 18.9 %all-to-all-start.1 = ((bf16[32,2,320]{2,1,0:T(2,128)(2,1)}), bf16[32,2,320]{2,1,0:T(2,128)(2,1)S(1)}, u32[]{:S(2)}, u32[]{:S(2)}) async-start(bf16[32,2,320]{2,1,0:T(2,128)(2,1)} %reshape.211), calls=%async_computation.1 | async-start | bytes 98304 | tf_op jit(solution)/shard_map/all_to_all | solution.py:85
  340.5 29.3 %copy-start.11 = (f32[3,512,32]{1,2,0:T(8,128)S(1)}, f32[3,512,32]{1,2,0:T(8,128)}, u32[]{:S(2)}) copy-start(f32[3,512,32]{1,2,0:T(8,128)} %param.11) | copy-start | bytes 589828
  348.6 17.3 %all-to-all-start.2 = ((bf16[32,2,320]{2,1,0:T(2,128)(2,1)}), bf16[32,2,320]{2,1,0:T(2,128)(2,1)S(1)}, u32[]{:S(2)}, u32[]{:S(2)}) async-start(bf16[32,2,320]{2,1,0:T(2,128)(2,1)} %reshape.209), calls=%async_computation.2 | async-start | bytes 98304 | tf_op jit(solution)/shard_map/all_to_all | solution.py:85
  365.9 16.1 %all-to-all-start = ((bf16[32,2,320]{2,1,0:T(2,128)(2,1)}), bf16[32,2,320]{2,1,0:T(2,128)(2,1)S(1)}, u32[]{:S(2)}, u32[]{:S(2)}) async-start(bf16[32,2,320]{2,1,0:T(2,128)(2,1)} %reshape.213), calls=%async_computation | async-start | bytes 98304 | tf_op jit(solution)/shard_map/all_to_all | solution.py:85
  369.8 378.8 %all-reduce.7.cloned.1.call-start = ((), (), s32[]{:S(2)}) async-start(), calls=%async_computation.6 | async-start | bytes 6291456 | tf_op jit(solution)/shard_map/psum | solution.py:104
  374.6 3.5 copy-start.7
  377.1 1.1 copy-start.9
  378.3 75.4 %copy-start.2 = (bf16[2,512,512]{2,1,0:T(8,128)(2,1)S(1)}, bf16[2,512,512]{2,1,0:T(8,128)(2,1)}, u32[]{:S(2)}) copy-start(bf16[2,512,512]{2,1,0:T(8,128)(2,1)} %param.10) | copy-start | bytes 3145732
  380.6 1.5 copy-start.5
  454.0 1.9 copy-start.8
  456.6 1.2 copy-start.10
  457.8 1.2 copy-start.6
  754.1 1.9 copy-start.4
  756.1 1.4 copy-start.1
Sparse Core Ops, SparseCore 0:
  57.7 86.3 all-gather.5
  147.3 79.8 all-gather.7
  230.9 79.7 all-gather.3
  318.3 133.3 all-reduce.8
  461.9 286.6 all-reduce.6
where the time goes:
time: 774 us; the launch traced here: 764 us
  waiting for transfers between devices  497 us (64%)
  local copies, waits for them, and re-layouts  86.5 us (11%)
  blocking collectives  73.4 us (9%)
  other arithmetic  50.2 us (6%)
  matrix products  25.9 us (3%)
  starting transfers between devices  15.7 us (2%)
  between operations  15.2 us (2%)
    psum x1, waiting for transfers between devices, per_device(): totals = lax.psum(jnp.stack(partial_list), ('row', 'col'))  285 us
    all_gather x3, waiting for transfers between devices, per_device(): column_full = lax.all_gather(column_part, 'row', axis=1, tiled=True)  125 us
    all_gather x3, blocking collectives, per_device(): lax.all_gather(flat[position:position + 1], 'col', axis=1, tiled=True)  73.4 us
    unnamed x6, waiting for transfers between devices  69.1 us
    all_gather x3, other arithmetic, per_device(): lax.all_gather(flat[position:position + 1], 'col', axis=1, tiled=True)  44.6 us
    another operation x9, local copies, waits for them, and re-layouts  32 us
    all_to_all x3, waiting for transfers between devices, per_device(): lax.all_to_all(outgoing, 'row', split_axis=1, concat_axis=1, tiled=True)  17.9 us
    all_to_all x3, starting transfers between devices, per_device(): lax.all_to_all(outgoing, 'row', split_axis=1, concat_axis=1, tiled=True)  15.5 us
  transfers between devices with their start and end apart: 8, of which 7 were waited for; matrix products, arithmetic and copies ran while one was open for 14% of the time, Pallas kernels for 0%

commit v1 on v0

v1 whole, which is shorter than its diff:
```python
import jax
import jax.numpy as jnp
from jax import lax
from jax.experimental import pallas as pl
from jax.experimental.pallas import tpu as pltpu
from jax.sharding import PartitionSpec as P

highest = lax.Precision.HIGHEST
MESH = pl.DeviceIdType.MESH
ZS, YH = 8, 4
CHIPS = 8


def greet(peers):
    barrier = pltpu.get_barrier_semaphore()
    for peer in peers:
        pl.semaphore_signal(barrier, inc=1, device_id=peer, device_id_type=MESH)
    pl.semaphore_wait(barrier, len(peers))


def push(src, dst, send_sem, recv_sem, device):
    return pltpu.make_async_remote_copy(
        src_ref=src,
        dst_ref=dst,
        send_sem=send_sem,
        recv_sem=recv_sem,
        device_id=device,
        device_id_type=MESH,
    )


def gather_col_kernel(x_ref, out_ref, local_sem, send_sem, pass_sem, recv_sem):
    row, col = lax.axis_index("row"), lax.axis_index("col")
    chip, core = col // 2, lax.rem(col, 2)
    partner = (row, chip * 2 + 1 - core)
    chips = [lax.rem(chip + j, CHIPS) for j in range(1, CHIPS)]
    greet([(row, other * 2 + core) for other in chips] + [partner])
    mine = pltpu.make_async_copy(x_ref, out_ref.at[col], local_sem)
    mine.start()
    copies = []
    for j, other in enumerate(chips):
        copies.append(push(x_ref, out_ref.at[col], send_sem.at[j], recv_sem.at[col], (row, other * 2 + core)))
    copies.append(push(x_ref, out_ref.at[col], pass_sem.at[0], recv_sem.at[col], partner))
    for copy in copies:
        copy.start()
    for j in range(1, CHIPS):
        other = lax.rem(chip + CHIPS - j, CHIPS)
        slot = other * 2 + core
        landed = push(x_ref, out_ref.at[slot], pass_sem.at[j], recv_sem.at[slot], partner)
        landed.wait_recv()
        onward = push(out_ref.at[slot], out_ref.at[slot], pass_sem.at[j], recv_sem.at[slot], partner)
        onward.start()
        copies.append(onward)
    for j in range(CHIPS):
        slot = lax.rem(chip + j, CHIPS) * 2 + 1 - core
        push(x_ref, out_ref.at[slot], pass_sem.at[0], recv_sem.at[slot], partner).wait_recv()
    for copy in copies:
        copy.wait_send()
    mine.wait()


def gather_col(x):
    return pl.pallas_call(
        gather_col_kernel,
        out_shape=jax.ShapeDtypeStruct((CHIPS * 2,) + x.shape, x.dtype),
        in_specs=[pl.BlockSpec(memory_space=pl.ANY)],
        out_specs=pl.BlockSpec(memory_space=pl.ANY),
        scratch_shapes=[
            pltpu.SemaphoreType.DMA,
            pltpu.SemaphoreType.DMA((CHIPS - 1,)),
            pltpu.SemaphoreType.DMA((CHIPS,)),
            pltpu.SemaphoreType.DMA((CHIPS * 2,)),
        ],
        compiler_params=pltpu.CompilerParams(collective_id=0, has_side_effects=True),
        name="gather_col",
    )(x)


def gather_row_kernel(x_ref, out_ref, local_sem, y_sem, z_sem, recv_sem):
    row, col = lax.axis_index("row"), lax.axis_index("col")
    z, y = row // YH, lax.rem(row, YH)
    right = (lax.rem(z + 1, ZS) * YH + y, col)
    left = (lax.rem(z + ZS - 1, ZS) * YH + y, col)
    others = [(z * YH + lax.rem(y + j, YH), col) for j in range(1, YH)]
    greet(others + [right, left])
    mine = pltpu.make_async_copy(x_ref, out_ref.at[:, row], local_sem)
    mine.start()
    copies = []

    def send(src, slot, sem, device):
        copy = push(src, out_ref.at[:, slot], sem, recv_sem.at[slot], device)
        copy.start()
        copies.append(copy)

    def arrive(slot):
        push(x_ref, out_ref.at[:, slot], local_sem, recv_sem.at[slot], right).wait_recv()

    send(x_ref, row, z_sem.at[0, 0, 0], right)
    send(x_ref, row, z_sem.at[1, 0, 0], left)
    for j in range(1, YH):
        send(x_ref, row, y_sem.at[j - 1], others[j - 1])
    for j in range(1, YH):
        slot = z * YH + lax.rem(y + j, YH)
        arrive(slot)
        send(out_ref.at[:, slot], slot, z_sem.at[0, j, 0], right)
        send(out_ref.at[:, slot], slot, z_sem.at[1, j, 0], left)
    for hop in range(1, ZS // 2 + 1):
        for j in range(YH):
            lane = lax.rem(y + j, YH)
            far_right = ZS // 2 - j % 2
            for way, far, at, device in (
                (0, far_right, lax.rem(z + ZS - hop, ZS), right),
                (1, ZS - 1 - far_right, lax.rem(z + hop, ZS), left),
            ):
                slot = at * YH + lane
                if hop <= far:
                    arrive(slot)
                if hop < far:
                    send(out_ref.at[:, slot], slot, z_sem.at[way, j, hop], device)
    for copy in copies:
        copy.wait_send()
    mine.wait()


def gather_row(x):
    supers, width_part, span = x.shape
    return pl.pallas_call(
        gather_row_kernel,
        out_shape=jax.ShapeDtypeStruct((supers, ZS * YH, width_part, span), x.dtype),
        in_specs=[pl.BlockSpec(memory_space=pl.ANY)],
        out_specs=pl.BlockSpec(memory_space=pl.ANY),
        scratch_shapes=[
            pltpu.SemaphoreType.DMA,
            pltpu.SemaphoreType.DMA((YH - 1,)),
            pltpu.SemaphoreType.DMA((2, YH, ZS // 2)),
            pltpu.SemaphoreType.DMA((ZS * YH,)),
        ],
        compiler_params=pltpu.CompilerParams(collective_id=1, has_side_effects=True),
        name="gather_row",
    )(x)


def swap_core_kernel(x_ref, out_ref, send_sem, recv_sem):
    row, col = lax.axis_index("row"), lax.axis_index("col")
    chip, core = col // 2, lax.rem(col, 2)
    partner = (row, chip * 2 + 1 - core)
    greet([partner])
    copy = push(x_ref.at[:, 1 - core], out_ref, send_sem, recv_sem, partner)
    copy.start()
    copy.wait()


def swap_core(x, ident):
    return pl.pallas_call(
        swap_core_kernel,
        out_shape=jax.ShapeDtypeStruct(x.shape[:1] + x.shape[2:], x.dtype),
        in_specs=[pl.BlockSpec(memory_space=pl.ANY)],
        out_specs=pl.BlockSpec(memory_space=pl.ANY),
        scratch_shapes=[pltpu.SemaphoreType.DMA, pltpu.SemaphoreType.DMA],
        compiler_params=pltpu.CompilerParams(collective_id=ident, has_side_effects=True),
        name="swap_core_%d" % ident,
    )(x)


def swap_chips_kernel(x_ref, out_ref, local_sem, send_sem, recv_sem):
    row, col = lax.axis_index("row"), lax.axis_index("col")
    chip, core = col // 2, lax.rem(col, 2)
    chips = [lax.rem(chip + j, CHIPS) for j in range(1, CHIPS)]
    greet([(row, other * 2 + core) for other in chips])
    mine = pltpu.make_async_copy(x_ref.at[chip], out_ref.at[chip], local_sem)
    mine.start()
    copies = [
        push(x_ref.at[other], out_ref.at[chip], send_sem.at[j], recv_sem.at[chip], (row, other * 2 + core))
        for j, other in enumerate(chips)
    ]
    for copy in copies:
        copy.start()
    for j, other in enumerate(chips):
        push(x_ref.at[other], out_ref.at[other], send_sem.at[j], recv_sem.at[other], (row, other * 2 + core)).wait_recv()
    for copy in copies:
        copy.wait_send()
    mine.wait()


def swap_chips(x, ident):
    return pl.pallas_call(
        swap_chips_kernel,
        out_shape=jax.ShapeDtypeStruct(x.shape, x.dtype),
        in_specs=[pl.BlockSpec(memory_space=pl.ANY)],
        out_specs=pl.BlockSpec(memory_space=pl.ANY),
        scratch_shapes=[
            pltpu.SemaphoreType.DMA,
            pltpu.SemaphoreType.DMA((CHIPS - 1,)),
            pltpu.SemaphoreType.DMA((CHIPS,)),
        ],
        compiler_params=pltpu.CompilerParams(collective_id=ident, has_side_effects=True),
        name="swap_chips_%d" % ident,
    )(x)


def scatter_sum(x, core, ident):
    grid = x.reshape((CHIPS, 2) + x.shape[1:])
    other = swap_core(grid, ident)
    own = lax.dynamic_index_in_dim(grid, core, 1, keepdims=False)
    return jnp.sum(swap_chips(own + other, ident + 1), axis=0)


def place_kernel(row_block_ref, occupancy_ref, column_ref, blocks_ref, placed_ref, part_ref):
    supers, nblocks = placed_ref.shape[:2]
    per = blocks_ref.shape[2]
    for s in range(supers):

        def step(device, carry, s=s):
            for k in range(per):
                b = device * per + k
                block = blocks_ref[device, s, k]
                keep = occupancy_ref[s, b] > 0
                placed_ref[s, row_block_ref[s, b]] = jnp.where(keep, block, jnp.zeros_like(block))
            return carry

        lax.fori_loop(0, nblocks // per, step, 0)
    first = column_ref[0] * per
    for s in range(supers):
        for k in range(per):
            part_ref[s, :, k * 128 : (k + 1) * 128] = placed_ref[s, first + k]


def place(blocks, occupancy, row_block, column):
    devices, supers, per, width_part, tall = blocks.shape
    smem = pl.BlockSpec(memory_space=pltpu.SMEM)
    vmem = pl.BlockSpec(memory_space=pltpu.VMEM)
    return pl.pallas_call(
        place_kernel,
        out_shape=(
            jax.ShapeDtypeStruct((supers, devices * per, width_part, tall), blocks.dtype),
            jax.ShapeDtypeStruct((supers, width_part, per * tall), blocks.dtype),
        ),
        in_specs=[smem, smem, smem, vmem],
        out_specs=(vmem, vmem),
        name="place",
    )(row_block, occupancy, column.reshape(1).astype(jnp.int32), blocks)


def dot_high(a, b):
    return jnp.dot(a, b, precision=highest)


def per_device(inverse_block, factor_cols, occupancy, row_block, coupling, diag_inverse):
    column = lax.axis_index("col")
    core = lax.rem(column, 2)
    row_first = (lax.axis_index("row") == 0).astype(jnp.float32)
    row_parts = lax.axis_size("row")
    col_parts = lax.axis_size("col")
    local_rows = inverse_block.shape[0]
    rows_total = local_rows * row_parts
    supers, span, width_part = factor_cols.shape
    width = width_part * row_parts
    tile = local_rows // col_parts
    diag_cols = diag_inverse.shape[2]
    per = span // 128

    packed = jnp.transpose(factor_cols.reshape(supers, per, 128, width_part), (0, 1, 3, 2))
    placed, part = place(gather_col(packed), occupancy, row_block, column)

    per_row = local_rows // 128
    block_at = jnp.minimum(column * tile // 128, per_row - 2)
    near = lax.dynamic_slice_in_dim(
        placed.reshape(supers, row_parts, per_row, width_part, 128), block_at, 2, 2
    )
    near = jnp.transpose(near, (0, 1, 3, 2, 4)).reshape(supers, row_parts, width_part, 256)
    outgoing = lax.dynamic_slice_in_dim(near, column * tile - block_at * 128, tile, 3)
    arrived = lax.all_to_all(outgoing, "row", split_axis=1, concat_axis=1, tiled=True)
    own_rows = arrived.reshape(supers, width, tile).astype(jnp.float32)

    panel = gather_row(part).reshape(supers * width, span)
    term = lax.dot_general(
        inverse_block, panel, (((1,), (1,)), ((), ())), preferred_element_type=jnp.float32
    )
    summed = scatter_sum(term.reshape(col_parts, tile, supers * width), core, 2)

    columns = []
    chain = []
    for s in range(supers):
        product = summed[:, s * width : (s + 1) * width]
        own = own_rows[s]
        if s == 0:
            current = -product
            inner = dot_high(current.T, own.T)
        else:
            link = coupling[s - 1].astype(jnp.float32)
            coupled = dot_high(columns[-1], link)
            current = -(product + coupled)
            inner = dot_high(current.T, own.T) - dot_high(own, coupled)
        embedded = lax.dynamic_update_slice(
            jnp.zeros((width, width), jnp.float32), diag_inverse[s].T, (column * diag_cols, 0)
        )
        total = row_first * embedded - inner / rows_total
        if s > 0:
            total = total + dot_high(link.T, dot_high(chain[-1], link))
        columns.append(current)
        chain.append(total)
    partial = jnp.stack([t.reshape(col_parts, diag_cols, width) for t in chain], axis=1)
    mine = scatter_sum(partial.reshape(col_parts, supers * diag_cols, width), core, 4)
    diagonals = jnp.transpose(lax.psum(mine, "row").reshape(supers, diag_cols, width), (0, 2, 1))
    return (jnp.stack(columns), diagonals)


def solution(mesh):
    in_specs = (P("row", "col"), P(None, "col", "row"), P(), P(), P(), P(None, None, "col"))
    out_specs = (P(None, ("row", "col"), None), P(None, None, "col"))
    return jax.shard_map(
        per_device, mesh=mesh, in_specs=in_specs, out_specs=out_specs, check_vma=False
    )
```

time: 774 us -> 535 us (0.69); the launches traced: 764 us -> 535 us
  waiting for transfers between devices: 497 us -> 306 us
  Pallas kernels: 0 us -> 153 us
  local copies, waits for them, and re-layouts: 86.5 us -> 13 us
  blocking collectives: 73.4 us -> 0 us
  other arithmetic: 50.2 us -> 13.7 us
    pallas_call x0 -> x7, Pallas kernels: none -> 153 us  [the longest x2 61.7 us: swap_chips(): pl.pallas_call(swap_chips_kernel, out_shape=jax.ShapeDtypeStruct(x.shape,...]
    all_gather x3 -> x0, waiting for transfers between devices: 125 us -> none  [per_device(): column_full = lax.all_gather(column_part, 'row', axis=1, tiled=True)]
    all_gather x3 -> x0, blocking collectives: 73.4 us -> none  [per_device(): lax.all_gather(flat[position:position + 1], 'col', axis=1, tiled=True)]
    unnamed x6 -> x1, waiting for transfers between devices: 69.1 us -> 0.02 us
    all_gather x3 -> x0, other arithmetic: 44.6 us -> none  [per_device(): lax.all_gather(flat[position:position + 1], 'col', axis=1, tiled=True)]
    another operation x12 -> x3, local copies, waits for them, and re-layouts: 44.4 us -> 2.31 us
    psum x1, waiting for transfers between devices: 285 us -> 306 us  [per_device(): lax.psum(mine, 'row').reshape(supers, diag_cols, width)]
    all_to_all x3 -> x1, waiting for transfers between devices: 17.9 us -> 0.01 us  [per_device(): lax.all_to_all(outgoing, 'row', split_axis=1, concat_axis=1, tiled=True)]
  transfers between devices with their start and end apart: 8 -> 2, of which waited for: 7 -> 1; matrix products, arithmetic and copies ran while one was open for 14% -> 3% of each run, Pallas kernels for 0% -> 18%
where the time goes in v1:
time: 535 us
  waiting for transfers between devices  306 us (57%)
  Pallas kernels  153 us (29%)
  matrix products  18.6 us (3%)
  starting transfers between devices  16.3 us (3%)
  between operations  14.4 us (3%)
  other arithmetic  13.7 us (3%)
  local copies, waits for them, and re-layouts  13 us (2%)
    psum x1, waiting for transfers between devices, per_device(): lax.psum(mine, 'row').reshape(supers, diag_cols, width)  306 us
    pallas_call x2, Pallas kernels, swap_chips(): pl.pallas_call(swap_chips_kernel, out_shape=jax.ShapeDtypeStruct(x.shape,...  61.7 us
    pallas_call x1, Pallas kernels, gather_row(): pl.pallas_call(gather_row_kernel, out_shape=jax.ShapeDtypeStruct((supers,...  57.1 us
    pallas_call x1, Pallas kernels, gather_col(): pl.pallas_call(gather_col_kernel, out_shape=jax.ShapeDtypeStruct((CHIPS *...  19.7 us
    all_to_all x1, starting transfers between devices, per_device(): lax.all_to_all(outgoing, 'row', split_axis=1, concat_axis=1, tiled=True)  16.1 us
    dot_general x11, matrix products, dot_high(): return jnp.dot(a, b, precision=highest)  11.9 us
  transfers between devices with their start and end apart: 2, of which 1 were waited for; matrix products, arithmetic and copies ran while one was open for 3% of the time, Pallas kernels for 18%

profile of v1, /device:TPU:6, one launch (start us, length us, event | category | flops | bytes accessed | tf_op | source)
XLA Modules:
  0.0 534.5 jit_solution(6995851375108319152)
XLA Ops:
  7.2 0.0 copy-start
  7.2 1.7 bitcast_bitcast_fusion.x_ref
  8.9 19.7 %gather_col.1.blocks_ref = bf16[16,3,10,16,128]{4,3,2,1,0:T(8,128)(2,1)} custom-call(bf16[3,10,16,128]{3,2,1,0:T(8,128)(2,1)} %bitcast_bitcast_fusion.x_ref), custom_call_target="tpu_custom_call" | custom-call | tf_op jit(solution)/shard_map/gather_col/pallas_call | solution.py:63
  28.6 4.7 place.1
  33.4 1.2 constant_dynamic-slice_fusion.1
  34.6 0.7 copy.27
  35.3 0.5 reshape.33
  35.8 0.2 copy_bitcast_fusion.1
  36.0 1.1 reshape.35
  37.1 16.1 %all-to-all-start = ((bf16[32,2,960]{2,1,0:T(2,128)(2,1)}), bf16[32,2,960]{2,1,0:T(2,128)(2,1)}, u32[]{:S(2)}, u32[]{:S(2)}) async-start(bf16[32,2,960]{2,1,0:T(2,128)(2,1)} %reshape.35), calls=%async_computation | async-start | bytes 262144 | tf_op jit(solution)/shard_map/all_to_all | solution.py:272
  53.1 0.2 all-reduce.2.cloned.1.call-start
  53.4 57.1 %gather_row.1 = bf16[3,32,16,1280]{3,2,1,0:T(8,128)(2,1)} custom-call(bf16[3,16,1280]{2,1,0:T(8,128)(2,1)} %get-tuple-element.4.x_ref), custom_call_target="tpu_custom_call" | custom-call | tf_op jit(solution)/shard_map/gather_row/pallas_call | solution.py:127
  110.5 0.0 copy-done
  110.5 6.7 %fusion.34 = f32[1536,640]{0,1:T(8,128)} fusion(bf16[1536,1280]{1,0:T(8,128)(2,1)} %bitcast.95, bf16[640,1280]{1,0:T(8,128)(2,1)S(1)} %copy-done), kind=kOutput, calls=%fused_computation.51 | convolution fusion | flops 2516582400 | bytes 9502720 | tf_op jit(solution)/shard_map/dot_general | solution.py:276
  117.2 5.0 swap_core_2.1
  122.3 3.7 bitcast_add_fusion.x_ref
  126.0 0.0 copy-start.3
  126.0 34.1 %swap_chips_3.1 = f32[8,40,1536]{2,1,0:T(8,128)} custom-call(f32[8,40,1536]{2,1,0:T(8,128)} %bitcast_add_fusion.x_ref), custom_call_target="tpu_custom_call" | custom-call | tf_op jit(solution)/shard_map/swap_chips_3/pallas_call | solution.py:186
  160.1 0.1 broadcast.11.clone
  160.2 0.0 copy-done.3
  160.2 0.0 copy-start.2
  160.2 1.0 copy-done.2
  161.2 1.1 broadcast.11.clone.1
  162.3 0.0 copy-start.1
  162.3 0.6 bitcast_dynamic-update-slice_fusion.1
  162.9 1.1 broadcast.11.clone.2
  164.0 0.6 bitcast_dynamic-update-slice_fusion
  164.6 1.7 reduce_sum.18
  166.3 0.0 copy-done.1
  166.3 0.4 fusion.15
  166.7 0.4 fusion.10
  167.1 0.0 all-to-all-done
  167.1 1.4 reshape.36
  168.5 1.9 fusion
  170.4 1.0 fusion.13
  171.4 1.1 convolution_bitcast_fusion.1
  172.5 0.6 fusion.29
  173.1 1.9 fusion.3
  175.1 1.0 fusion.8
  176.1 1.1 convolution_bitcast_fusion
  177.1 0.6 fusion.26
  177.8 1.9 fusion.6
  179.7 2.0 pad_maximum_fusion
  181.7 4.5 swap_core_4.1
  186.2 3.4 bitcast_add_fusion.1.x_ref
  189.5 27.6 %swap_chips_5.1 = f32[8,96,512]{2,1,0:T(8,128)} custom-call(f32[8,96,512]{2,1,0:T(8,128)} %bitcast_add_fusion.1.x_ref), custom_call_target="tpu_custom_call" | custom-call | tf_op jit(solution)/shard_map/swap_chips_5/pallas_call | solution.py:186
  217.2 2.2 reduce_sum.19
  219.4 0.0 all-reduce.2.cloned.1.call-update
  219.5 0.7 pad_maximum_fusion.1
  220.2 305.9 %all-reduce.2.cloned.1.call-done = f32[3,512,32]{1,2,0:T(8,128)} async-done(((f32[3,512,32]{1,2,0:T(8,128)}), f32[3,512,32]{1,2,0:T(8,128)}) %all-reduce.2.cloned.1.call-update) | async-done | bytes 196624 | tf_op jit(solution)/shard_map/psum | solution.py:304
  526.0 1.6 copy.34
  (3 shorter events, 0.1 us)
Async XLA Ops:
  7.2 103.3 %copy-start = (bf16[640,1280]{1,0:T(8,128)(2,1)S(1)}, bf16[640,1280]{1,0:T(8,128)(2,1)}, u32[]{:S(2)}) copy-start(bf16[640,1280]{1,0:T(8,128)(2,1)} %param.6) | copy-start | bytes 4915204
  37.1 130.0 %all-to-all-start = ((bf16[32,2,960]{2,1,0:T(2,128)(2,1)}), bf16[32,2,960]{2,1,0:T(2,128)(2,1)}, u32[]{:S(2)}, u32[]{:S(2)}) async-start(bf16[32,2,960]{2,1,0:T(2,128)(2,1)} %reshape.35), calls=%async_computation | async-start | bytes 262144 | tf_op jit(solution)/shard_map/all_to_all | solution.py:272
  53.1 472.9 %all-reduce.2.cloned.1.call-start = ((), (), s32[]{:S(2)}) async-start(), calls=%async_computation.1 | async-start | bytes 393216 | tf_op jit(solution)/shard_map/psum | solution.py:304
  126.0 34.2 %copy-start.3 = (f32[3,512,32]{1,2,0:T(8,128)S(1)}, f32[3,512,32]{1,2,0:T(8,128)}, u32[]{:S(2)}) copy-start(f32[3,512,32]{1,2,0:T(8,128)} %param.11) | copy-start | bytes 589828
  160.2 1.0 copy-start.2
  162.3 4.0 copy-start.1
Sparse Core Ops, SparseCore 0:
  219.5 306.4 all-reduce.1

commit v2 on v1

--- a/solution.py
+++ b/solution.py
@@ -8,7 +8,7 @@
 highest = lax.Precision.HIGHEST
 MESH = pl.DeviceIdType.MESH
 ZS, YH = 8, 4
-CHIPS = 8
+CHIPS, XS = 8, 4
 
 
 def greet(peers):
@@ -29,31 +29,58 @@
     )
 
 
-def gather_col_kernel(x_ref, out_ref, local_sem, send_sem, pass_sem, recv_sem):
+def ring_position():
     row, col = lax.axis_index("row"), lax.axis_index("col")
     chip, core = col // 2, lax.rem(col, 2)
+    x, y = lax.rem(chip, XS), chip // XS
+
+    def at(dx, dy):
+        return (y if dy == 0 else 1 - y) * XS + lax.rem(x + dx, XS)
+
+    return row, core, at
+
+
+NEAR = ((1, 0), (XS - 1, 0), (0, 1), (1, 1), (XS - 1, 1))
+
+
+def gather_col_kernel(x_ref, out_ref, local_sem, send_sem, pass_sem, turn_sem, half_sem, recv_sem):
+    row, core, at = ring_position()
+    chip = at(0, 0)
+    col = chip * 2 + core
     partner = (row, chip * 2 + 1 - core)
-    chips = [lax.rem(chip + j, CHIPS) for j in range(1, CHIPS)]
-    greet([(row, other * 2 + core) for other in chips] + [partner])
+    half = x_ref.shape[0] // 2
+    parts = (pl.ds(0, half), pl.ds(half, x_ref.shape[0] - half))
+    greet([(row, at(*step) * 2 + core) for step in NEAR] + [partner])
     mine = pltpu.make_async_copy(x_ref, out_ref.at[col], local_sem)
     mine.start()
     copies = []
-    for j, other in enumerate(chips):
-        copies.append(push(x_ref, out_ref.at[col], send_sem.at[j], recv_sem.at[col], (row, other * 2 + core)))
-    copies.append(push(x_ref, out_ref.at[col], pass_sem.at[0], recv_sem.at[col], partner))
-    for copy in copies:
+
+    def send(src, dst, sem, landing, device):
+        copy = push(src, dst, sem, landing, device)
         copy.start()
-    for j in range(1, CHIPS):
-        other = lax.rem(chip + CHIPS - j, CHIPS)
-        slot = other * 2 + core
-        landed = push(x_ref, out_ref.at[slot], pass_sem.at[j], recv_sem.at[slot], partner)
-        landed.wait_recv()
-        onward = push(out_ref.at[slot], out_ref.at[slot], pass_sem.at[j], recv_sem.at[slot], partner)
-        onward.start()
-        copies.append(onward)
-    for j in range(CHIPS):
-        slot = lax.rem(chip + j, CHIPS) * 2 + 1 - core
-        push(x_ref, out_ref.at[slot], pass_sem.at[0], recv_sem.at[slot], partner).wait_recv()
+        copies.append(copy)
+
+    for j, step in enumerate(NEAR):
+        send(x_ref, out_ref.at[col], send_sem.at[j], recv_sem.at[col], (row, at(*step) * 2 + core))
+    send(x_ref, out_ref.at[col], pass_sem.at[0], recv_sem.at[col], partner)
+    for j, step in enumerate(NEAR):
+        slot = at(*step) * 2 + core
+        push(x_ref, out_ref.at[slot], local_sem, recv_sem.at[slot], partner).wait_recv()
+        if step[1] == 0:
+            piece = out_ref.at[slot, parts[j]]
+            for dy in range(2):
+                device = (row, at(XS - step[0], dy) * 2 + core)
+                send(piece, piece, turn_sem.at[j, dy], half_sem.at[j, dy], device)
+        send(out_ref.at[slot], out_ref.at[slot], pass_sem.at[1 + j], recv_sem.at[slot], partner)
+    for dy in range(2):
+        slot = at(2, dy) * 2 + core
+        for j in range(2):
+            piece = out_ref.at[slot, parts[j]]
+            push(piece, piece, local_sem, half_sem.at[j, dy], partner).wait_recv()
+        send(out_ref.at[slot], out_ref.at[slot], pass_sem.at[6 + dy], recv_sem.at[slot], partner)
+    for step in ((0, 0),) + NEAR + ((2, 0), (2, 1)):
+        slot = at(*step) * 2 + 1 - core
+        push(x_ref, out_ref.at[slot], local_sem, recv_sem.at[slot], partner).wait_recv()
     for copy in copies:
         copy.wait_send()
     mine.wait()
@@ -67,8 +94,10 @@
         out_specs=pl.BlockSpec(memory_space=pl.ANY),
         scratch_shapes=[
             pltpu.SemaphoreType.DMA,
-            pltpu.SemaphoreType.DMA((CHIPS - 1,)),
+            pltpu.SemaphoreType.DMA((len(NEAR),)),
             pltpu.SemaphoreType.DMA((CHIPS,)),
+            pltpu.SemaphoreType.DMA((2, 2)),
+            pltpu.SemaphoreType.DMA((2, 2)),
             pltpu.SemaphoreType.DMA((CHIPS * 2,)),
         ],
         compiler_params=pltpu.CompilerParams(collective_id=0, has_side_effects=True),
@@ -122,7 +151,7 @@
     mine.wait()
 
 
-def gather_row(x):
+def gather_row(x, ident):
     supers, width_part, span = x.shape
     return pl.pallas_call(
         gather_row_kernel,
@@ -135,8 +164,8 @@
             pltpu.SemaphoreType.DMA((2, YH, ZS // 2)),
             pltpu.SemaphoreType.DMA((ZS * YH,)),
         ],
-        compiler_params=pltpu.CompilerParams(collective_id=1, has_side_effects=True),
-        name="gather_row",
+        compiler_params=pltpu.CompilerParams(collective_id=ident, has_side_effects=True),
+        name="gather_row_%d" % ident,
     )(x)
 
 
@@ -162,40 +191,127 @@
     )(x)
 
 
-def swap_chips_kernel(x_ref, out_ref, local_sem, send_sem, recv_sem):
-    row, col = lax.axis_index("row"), lax.axis_index("col")
-    chip, core = col // 2, lax.rem(col, 2)
-    chips = [lax.rem(chip + j, CHIPS) for j in range(1, CHIPS)]
-    greet([(row, other * 2 + core) for other in chips])
+def swap_chips_kernel(x_ref, out_ref, relay, local_sem, send_sem, away_sem, turn_sem, relay_sem, half_sem, recv_sem):
+    row, core, at = ring_position()
+    chip = at(0, 0)
+    rows = x_ref.shape[1]
+    cut = rows // 16 * 8
+    parts = (pl.ds(0, cut), pl.ds(cut, rows - cut))
+    sizes = (cut, rows - cut)
+
+    def device(step):
+        return (row, at(*step) * 2 + core)
+
+    greet([device(step) for step in NEAR])
     mine = pltpu.make_async_copy(x_ref.at[chip], out_ref.at[chip], local_sem)
     mine.start()
-    copies = [
-        push(x_ref.at[other], out_ref.at[chip], send_sem.at[j], recv_sem.at[chip], (row, other * 2 + core))
-        for j, other in enumerate(chips)
-    ]
-    for copy in copies:
+    copies = []
+
+    def send(src, dst, sem, landing, device):
+        copy = push(src, dst, sem, landing, device)
         copy.start()
-    for j, other in enumerate(chips):
-        push(x_ref.at[other], out_ref.at[other], send_sem.at[j], recv_sem.at[other], (row, other * 2 + core)).wait_recv()
+        copies.append(copy)
+
+    def held(j, dy):
+        return relay.at[j, dy, pl.ds(0, sizes[j])]
+
+    for dy in range(2):
+        for j in range(2):
+            send(x_ref.at[at(2, dy), parts[j]], held(j, dy), away_sem.at[j, dy], relay_sem.at[j, dy], device(NEAR[j]))
+    for j, step in enumerate(NEAR):
+        send(x_ref.at[at(*step)], out_ref.at[chip], send_sem.at[j], recv_sem.at[chip], device(step))
+    for dy in range(2):
+        for j in range(2):
+            origin = at(XS - NEAR[j][0], 0)
+            push(held(j, dy), held(j, dy), local_sem, relay_sem.at[j, dy], device(NEAR[j])).wait_recv()
+            target = device((NEAR[j][0], dy))
+            send(held(j, dy), out_ref.at[origin, parts[j]], turn_sem.at[j, dy], half_sem.at[j, dy], target)
+    for step in NEAR:
+        other = at(*step)
+        push(x_ref.at[other], out_ref.at[other], local_sem, recv_sem.at[other], device(step)).wait_recv()
+    for dy in range(2):
+        for j in range(2):
+            piece = out_ref.at[at(2, dy), parts[j]]
+            push(piece, piece, local_sem, half_sem.at[j, dy], device(NEAR[0])).wait_recv()
     for copy in copies:
         copy.wait_send()
     mine.wait()
 
 
 def swap_chips(x, ident):
+    chips, rows, lanes = x.shape
+    four = pltpu.SemaphoreType.DMA((2, 2))
     return pl.pallas_call(
         swap_chips_kernel,
         out_shape=jax.ShapeDtypeStruct(x.shape, x.dtype),
         in_specs=[pl.BlockSpec(memory_space=pl.ANY)],
         out_specs=pl.BlockSpec(memory_space=pl.ANY),
         scratch_shapes=[
+            pltpu.VMEM((2, 2, rows - rows // 16 * 8, lanes), x.dtype),
             pltpu.SemaphoreType.DMA,
-            pltpu.SemaphoreType.DMA((CHIPS - 1,)),
-            pltpu.SemaphoreType.DMA((CHIPS,)),
+            pltpu.SemaphoreType.DMA((len(NEAR),)),
+            four,
+            four,
+            four,
+            four,
+            pltpu.SemaphoreType.DMA((chips,)),
         ],
         compiler_params=pltpu.CompilerParams(collective_id=ident, has_side_effects=True),
         name="swap_chips_%d" % ident,
     )(x)
+
+
+def swap_row_kernel(along_z, x_ref, out_ref, local_sem, send_sem, recv_sem):
+    row, col = lax.axis_index("row"), lax.axis_index("col")
+    z, y = row // YH, lax.rem(row, YH)
+    count = x_ref.shape[0]
+    me = z if along_z else y
+    others = [lax.rem(me + j, count) for j in range(1, count)]
+    devices = [(other * YH + y if along_z else z * YH + other, col) for other in others]
+    greet(devices)
+    mine = pltpu.make_async_copy(x_ref.at[me], out_ref.at[me], local_sem)
+    mine.start()
+    copies = [
+        push(x_ref.at[other], out_ref.at[me], send_sem.at[j], recv_sem.at[me], devices[j])
+        for j, other in enumerate(others)
+    ]
+    for copy in copies:
+        copy.start()
+    for j, other in enumerate(others):
+        push(x_ref.at[other], out_ref.at[other], send_sem.at[j], recv_sem.at[other], devices[j]).wait_recv()
+    for copy in copies:
+        copy.wait_send()
+    mine.wait()
+
+
+def swap_row(x, along_z, ident):
+    count = x.shape[0]
+
+    def kernel(*refs):
+        swap_row_kernel(along_z, *refs)
+
+    return pl.pallas_call(
+        kernel,
+        out_shape=jax.ShapeDtypeStruct(x.shape, x.dtype),
+        in_specs=[pl.BlockSpec(memory_space=pl.ANY)],
+        out_specs=pl.BlockSpec(memory_space=pl.ANY),
+        scratch_shapes=[
+            pltpu.SemaphoreType.DMA,
+            pltpu.SemaphoreType.DMA((count - 1,)),
+            pltpu.SemaphoreType.DMA((count,)),
+        ],
+        compiler_params=pltpu.CompilerParams(collective_id=ident, has_side_effects=True),
+        name="swap_row_%d" % ident,
+    )(x)
+
+
+def sum_row(x, ident):
+    rows, lanes = x.shape
+    piece = jnp.sum(swap_row(x.reshape(YH, rows // YH, lanes), False, ident), axis=0)
+    piece = piece.reshape(ZS, rows // (YH * ZS), lanes)
+    piece = jnp.sum(swap_row(piece, True, ident + 1), axis=0)
+    whole = gather_row(piece[None], ident + 2).reshape(ZS, YH, -1, lanes)
+    return jnp.transpose(whole, (1, 0, 2, 3)).reshape(rows, lanes)
 
 
 def scatter_sum(x, core, ident):
@@ -272,7 +388,7 @@
     arrived = lax.all_to_all(outgoing, "row", split_axis=1, concat_axis=1, tiled=True)
     own_rows = arrived.reshape(supers, width, tile).astype(jnp.float32)
 
-    panel = gather_row(part).reshape(supers * width, span)
+    panel = gather_row(part, 1).reshape(supers * width, span)
     term = lax.dot_general(
         inverse_block, panel, (((1,), (1,)), ((), ())), preferred_element_type=jnp.float32
     )
@@ -301,7 +417,7 @@
         chain.append(total)
     partial = jnp.stack([t.reshape(col_parts, diag_cols, width) for t in chain], axis=1)
     mine = scatter_sum(partial.reshape(col_parts, supers * diag_cols, width), core, 4)
-    diagonals = jnp.transpose(lax.psum(mine, "row").reshape(supers, diag_cols, width), (0, 2, 1))
+    diagonals = jnp.transpose(sum_row(mine, 6).reshape(supers, diag_cols, width), (0, 2, 1))
     return (jnp.stack(columns), diagonals)
 
 

time: 535 us -> 254 us (0.47)
  waiting for transfers between devices: 306 us -> 0.01 us
  Pallas kernels: 153 us -> 185 us
  between operations: 14.4 us -> 0.95 us
    psum x1 -> x0, waiting for transfers between devices: 306 us -> none  [per_device(): lax.psum(mine, 'row').reshape(supers, diag_cols, width)]
    pallas_call x1 -> x2, Pallas kernels: 57.1 us -> 81.3 us  [gather_row(): pl.pallas_call(gather_row_kernel, out_shape=jax.ShapeDtypeStruct((supers,...]
    pallas_call x0 -> x2, Pallas kernels: none -> 19.7 us  [swap_row(): pl.pallas_call(kernel, out_shape=jax.ShapeDtypeStruct(x.shape, x.dtype),...]
    pallas_call x2, Pallas kernels: 61.7 us -> 51.6 us  [swap_chips(): pl.pallas_call(swap_chips_kernel, out_shape=jax.ShapeDtypeStruct(x.shape,...]
  transfers between devices with their start and end apart: 2 -> 1, of which waited for: 1 -> 0; matrix products, arithmetic and copies ran while one was open for 3% -> 8% of each run, Pallas kernels for 18% -> 36%
where the time goes in v2:
time: 254 us; the launch traced here: 253 us
  Pallas kernels  185 us (73%)
  matrix products  18.6 us (7%)
  local copies, waits for them, and re-layouts  17 us (7%)
  other arithmetic  16.2 us (6%)
  starting transfers between devices  15.5 us (6%)
    pallas_call x2, Pallas kernels, gather_row(): pl.pallas_call(gather_row_kernel, out_shape=jax.ShapeDtypeStruct((supers,...  81.3 us
    pallas_call x2, Pallas kernels, swap_chips(): pl.pallas_call(swap_chips_kernel, out_shape=jax.ShapeDtypeStruct(x.shape,...  51.6 us
    pallas_call x2, Pallas kernels, swap_row(): pl.pallas_call(kernel, out_shape=jax.ShapeDtypeStruct(x.shape, x.dtype),...  19.7 us
    pallas_call x1, Pallas kernels, gather_col(): pl.pallas_call(gather_col_kernel, out_shape=jax.ShapeDtypeStruct((CHIPS *...  17.8 us
    all_to_all x1, starting transfers between devices, per_device(): lax.all_to_all(outgoing, 'row', split_axis=1, concat_axis=1, tiled=True)  15.5 us
    dot_general x11, matrix products, dot_high(): return jnp.dot(a, b, precision=highest)  11.9 us
    pallas_call x2, Pallas kernels, swap_core(): pl.pallas_call(swap_core_kernel, out_shape=jax.ShapeDtypeStruct(x.shape[:...  9.51 us
    add x2, other arithmetic, scatter_sum(): return jnp.sum(swap_chips(own + other, ident + 1), axis=0)  7.08 us
  transfers between devices with their start and end apart: 1, of which 0 were waited for; matrix products, arithmetic and copies ran while one was open for 8% of the time, Pallas kernels for 36%

profile of v2, /device:TPU:6, one launch (start us, length us, event | category | flops | bytes accessed | tf_op | source)
XLA Modules:
  0.0 252.9 jit_solution(7274274706282316632)
XLA Ops:
  0.6 0.0 copy-start
  0.7 1.7 bitcast_bitcast_fusion.x_ref
  2.3 17.8 %gather_col.1.blocks_ref = bf16[16,3,10,16,128]{4,3,2,1,0:T(8,128)(2,1)} custom-call(bf16[3,10,16,128]{3,2,1,0:T(8,128)(2,1)} %bitcast_bitcast_fusion.x_ref), custom_call_target="tpu_custom_call" | custom-call | tf_op jit(solution)/shard_map/gather_col/pallas_call | solution.py:90
  20.1 4.7 %place.1 = (bf16[3,160,16,128]{3,2,1,0:T(8,128)(2,1)}, bf16[3,16,1280]{2,1,0:T(8,128)(2,1)}) custom-call(s32[3,160]{1,0:T(4,128)} %row_block_ref.1, s32[3,160]{1,0:T(4,128)} %occupancy_ref.1, s32[1]{0:T(128)} %bitcast.column_ref, bf16[16,3,10,16,128]{4,3,2,1,0:T(8,128)(2,1)} %gather_col.1.blocks_ref), custom_call_target="tpu_custom_call" | custom-call | tf_op jit(solution)/shard_map/place/pallas_call | solution.py:348
  24.9 1.2 constant_dynamic-slice_fusion.1
  26.1 0.7 copy.31
  26.8 0.5 reshape.39
  27.3 0.2 copy_bitcast_fusion.2
  27.5 1.1 reshape.43
  28.6 15.5 %all-to-all-start = ((bf16[32,2,960]{2,1,0:T(2,128)(2,1)}), bf16[32,2,960]{2,1,0:T(2,128)(2,1)}, u32[]{:S(2)}, u32[]{:S(2)}) async-start(bf16[32,2,960]{2,1,0:T(2,128)(2,1)} %reshape.43), calls=%async_computation | async-start | bytes 262144 | tf_op jit(solution)/shard_map/all_to_all | solution.py:388
  44.1 57.1 %gather_row_1.1 = bf16[3,32,16,1280]{3,2,1,0:T(8,128)(2,1)} custom-call(bf16[3,16,1280]{2,1,0:T(8,128)(2,1)} %get-tuple-element.4.x_ref), custom_call_target="tpu_custom_call" | custom-call | tf_op jit(solution)/shard_map/gather_row_1/pallas_call | solution.py:156
  101.2 0.0 copy-done
  101.2 6.7 %fusion.34 = f32[1536,640]{0,1:T(8,128)} fusion(bf16[1536,1280]{1,0:T(8,128)(2,1)} %bitcast.99, bf16[640,1280]{1,0:T(8,128)(2,1)S(1)} %copy-done), kind=kOutput, calls=%fused_computation.52 | convolution fusion | flops 2516582400 | bytes 9502720 | tf_op jit(solution)/shard_map/dot_general | solution.py:392
  107.9 5.0 %swap_core_2.1 = f32[8,40,1536]{2,1,0:T(8,128)} custom-call(f32[8,2,40,1536]{3,2,1,0:T(8,128)} %bitcast.96), custom_call_target="tpu_custom_call" | custom-call | tf_op jit(solution)/shard_map/swap_core_2/pallas_call | solution.py:183
  112.9 3.7 %bitcast_add_fusion.x_ref = f32[8,40,1536]{2,1,0:T(8,128)} fusion(f32[8,40,1536]{2,1,0:T(8,128)} %swap_core_2.1, f32[8,2,40,1536]{3,2,1,0:T(8,128)} %bitcast.97, s32[]{:T(128)S(6)} %select_n.22), kind=kLoop, calls=%fused_computation.1 | loop fusion | flops 491520 | bytes 5898244 | tf_op jit(solution)/shard_map/add | solution.py:321
  116.7 28.4 %swap_chips_3.1 = f32[8,40,1536]{2,1,0:T(8,128)} custom-call(f32[8,40,1536]{2,1,0:T(8,128)} %bitcast_add_fusion.x_ref), custom_call_target="tpu_custom_call" | custom-call | tf_op jit(solution)/shard_map/swap_chips_3/pallas_call | solution.py:244
  145.1 0.0 copy-start.1
  145.1 1.8 reduce_sum.36
  146.9 0.0 copy-done.1
  146.9 0.4 fusion.15
  147.3 0.4 fusion.10
  147.7 1.1 broadcast.11.clone
  148.8 1.5 bitcast_dynamic-update-slice_fusion.2
  150.3 1.2 broadcast.11.clone.1
  151.4 1.5 bitcast_dynamic-update-slice_fusion.1
  152.9 0.7 pad_maximum_fusion.1
  153.6 1.1 broadcast.11.clone.2
  154.7 1.5 bitcast_dynamic-update-slice_fusion
  156.2 0.0 all-to-all-done
  156.2 1.4 reshape.44
  157.6 1.9 fusion
  159.5 1.0 fusion.13
  160.5 1.1 convolution_bitcast_fusion.1
  161.6 0.6 fusion.29
  162.3 1.9 fusion.3
  164.2 1.0 fusion.8
  165.2 1.1 convolution_bitcast_fusion
  166.3 0.6 fusion.26
  166.9 1.9 fusion.6
  168.9 2.0 pad_maximum_fusion
  170.8 4.5 %swap_core_4.1 = f32[8,96,512]{2,1,0:T(8,128)} custom-call(f32[8,2,96,512]{3,2,1,0:T(8,128)} %bitcast.92), custom_call_target="tpu_custom_call" | custom-call | tf_op jit(solution)/shard_map/swap_core_4/pallas_call | solution.py:183
  175.3 3.4 %bitcast_add_fusion.1.x_ref = f32[8,96,512]{2,1,0:T(8,128)} fusion(f32[8,96,512]{2,1,0:T(8,128)} %swap_core_4.1, f32[8,2,96,512]{3,2,1,0:T(8,128)} %bitcast.93, s32[]{:T(128)S(6)} %select_n.22), kind=kLoop, calls=%fused_computation.2 | loop fusion | flops 393216 | bytes 4718596 | tf_op jit(solution)/shard_map/add | solution.py:321
  178.7 23.1 %swap_chips_5.1 = f32[8,96,512]{2,1,0:T(8,128)} custom-call(f32[8,96,512]{2,1,0:T(8,128)} %bitcast_add_fusion.1.x_ref), custom_call_target="tpu_custom_call" | custom-call | tf_op jit(solution)/shard_map/swap_chips_5/pallas_call | solution.py:244
  201.8 2.2 reduce_sum.37
  204.1 10.3 %swap_row_6.1 = f32[4,24,512]{2,1,0:T(8,128)} custom-call(f32[4,24,512]{2,1,0:T(8,128)} %bitcast.108), custom_call_target="tpu_custom_call" | custom-call | tf_op jit(solution)/shard_map/swap_row_6/pallas_call | solution.py:293
  214.4 0.9 reduce_sum.38
  215.3 0.7 reshape.41.refs_0_
  216.0 9.4 %swap_row_7.1 = f32[8,3,512]{2,1,0:T(4,128)} custom-call(f32[8,3,512]{2,1,0:T(4,128)} %reshape.41.refs_0_), custom_call_target="tpu_custom_call" | custom-call | tf_op jit(solution)/shard_map/swap_row_7/pallas_call | solution.py:293
  225.4 1.5 reduce_sum.39
  226.9 24.2 %gather_row_8.1 = f32[1,32,3,512]{3,2,1,0:T(4,128)} custom-call(f32[1,3,512]{2,1,0:T(4,128)} %bitcast.112), custom_call_target="tpu_custom_call" | custom-call | tf_op jit(solution)/shard_map/gather_row_8/pallas_call | solution.py:156
  251.1 1.0 copy.32
  252.1 0.8 reshape_reshape.11
  (2 shorter events, 0.1 us)
Async XLA Ops:
  0.6 100.5 %copy-start = (bf16[640,1280]{1,0:T(8,128)(2,1)S(1)}, bf16[640,1280]{1,0:T(8,128)(2,1)}, u32[]{:S(2)}) copy-start(bf16[640,1280]{1,0:T(8,128)(2,1)} %param.6) | copy-start | bytes 4915204
  28.6 127.6 %all-to-all-start = ((bf16[32,2,960]{2,1,0:T(2,128)(2,1)}), bf16[32,2,960]{2,1,0:T(2,128)(2,1)}, u32[]{:S(2)}, u32[]{:S(2)}) async-start(bf16[32,2,960]{2,1,0:T(2,128)(2,1)} %reshape.43), calls=%async_computation | async-start | bytes 262144 | tf_op jit(solution)/shard_map/all_to_all | solution.py:388
  145.1 1.8 copy-start.1

commit v3 on v2

--- a/solution.py
+++ b/solution.py
@@ -105,67 +105,185 @@
     )(x)
 
 
-def gather_row_kernel(x_ref, out_ref, local_sem, y_sem, z_sem, recv_sem):
+def gather_row_kernel(x_ref, rows_ref, out_ref, own_ref, staged, local_sem, send_sem, wide_sem, thin_sem, z_sem, y_sem):
     row, col = lax.axis_index("row"), lax.axis_index("col")
     z, y = row // YH, lax.rem(row, YH)
-    right = (lax.rem(z + 1, ZS) * YH + y, col)
-    left = (lax.rem(z + ZS - 1, ZS) * YH + y, col)
-    others = [(z * YH + lax.rem(y + j, YH), col) for j in range(1, YH)]
-    greet(others + [right, left])
-    mine = pltpu.make_async_copy(x_ref, out_ref.at[:, row], local_sem)
+    last = x_ref.shape[0] - 1
+    parts = (pl.ds(0, last), pl.ds(last, 1))
+    sems = (wide_sem, thin_sem)
+
+    def at(dz, dy):
+        return lax.rem(z + dz + ZS, ZS) * YH + lax.rem(y + dy + YH, YH)
+
+    def device(dz, dy):
+        return (at(dz, dy), col)
+
+    zs, ys = range(1, ZS), range(1, YH)
+    greet([device(dz, 0) for dz in zs] + [device(0, dy) for dy in ys])
+    locals_ = [pltpu.make_async_copy(x_ref, out_ref.at[:, row], local_sem.at[0])]
+    locals_.append(pltpu.make_async_copy(rows_ref.at[z], staged.at[z], local_sem.at[1]))
+    for copy in locals_:
+        copy.start()
+    copies = []
+
+    def send(src, dst, landing, where):
+        copy = push(src, dst, send_sem.at[len(copies)], landing, where)
+        copy.start()
+        copies.append(copy)
+
+    def block(kind, slot):
+        return out_ref.at[parts[kind], slot]
+
+    def onward(kind, slot, where, first=False):
+        src = x_ref.at[parts[kind]] if first else block(kind, slot)
+        send(src, block(kind, slot), sems[kind].at[slot], where)
+
+    def arrive(kind, slot):
+        piece = block(kind, slot)
+        push(piece, piece, local_sem.at[0], sems[kind].at[slot], device(1, 0)).wait_recv()
+
+    right, left, up, down = device(1, 0), device(-1, 0), device(0, 1), device(0, -1)
+    for where in (right, left):
+        onward(1, row, where, True)
+    for where in (up, down):
+        onward(0, row, where, True)
+    for where in (right, left):
+        onward(0, row, where, True)
+    for where in (up, down):
+        onward(1, row, where, True)
+    for dz in zs:
+        there = lax.rem(z + dz, ZS)
+        send(rows_ref.at[there], staged.at[z], z_sem.at[z], device(dz, 0))
+
+    for dy in (-1, 1, 2):
+        slot = at(0, dy)
+        arrive(0, slot)
+        if dy == -1:
+            onward(0, slot, up)
+        onward(0, slot, right)
+        onward(0, slot, left)
+
+    half = ZS // 2
+
+    def cross(dz):
+        arrive(1, at(dz, -1))
+        if dz % 2 == 0:
+            onward(1, at(dz, -1), up)
+        arrive(1, at(dz, 1))
+        if dz % 2 == 1:
+            onward(1, at(dz, 1), down)
+
+    for hop in range(1, half + 1):
+        for dz, far, where in ((-hop, half, right), (hop, ZS - 1 - half, left)):
+            if hop <= far:
+                slot = at(dz, 0)
+                arrive(1, slot)
+                if hop < far:
+                    onward(1, slot, where)
+                onward(1, slot, up)
+                onward(1, slot, down)
+        for j in range(YH):
+            far_right = half - j % 2
+            for dz, far, where in ((-hop, far_right, right), (hop, ZS - 1 - far_right, left)):
+                if hop <= far:
+                    arrive(0, at(dz, j))
+                if hop < far:
+                    onward(0, at(dz, j), where)
+        cross(hop - 1)
+        if hop > 1:
+            cross(1 - hop)
+        if hop == 1:
+            locals_[1].wait()
+            for dz in zs:
+                there = lax.rem(z + dz, ZS)
+                push(rows_ref.at[there], staged.at[there], local_sem.at[1], z_sem.at[there], right).wait_recv()
+            keep = pltpu.make_async_copy(staged.at[:, y], own_ref.at[:, y], local_sem.at[1])
+            keep.start()
+            for dy in ys:
+                there = lax.rem(y + dy, YH)
+                send(staged.at[:, there], own_ref.at[:, y], y_sem.at[y], device(0, dy))
+    cross(half)
+    for dz in range(1 - half, half + 1):
+        arrive(1, at(dz, 2))
+    for dy in ys:
+        there = lax.rem(y + dy, YH)
+        push(staged.at[:, there], own_ref.at[:, there], local_sem.at[1], y_sem.at[there], right).wait_recv()
+    for copy in copies:
+        copy.wait_send()
+    locals_[0].wait()
+    keep.wait()
+
+
+def gather_row(x, rows):
+    supers, width_part, span = x.shape
+    any_space = pl.BlockSpec(memory_space=pl.ANY)
+    return pl.pallas_call(
+        gather_row_kernel,
+        out_shape=(
+            jax.ShapeDtypeStruct((supers, ZS * YH, width_part, span), x.dtype),
+            jax.ShapeDtypeStruct(rows.shape, rows.dtype),
+        ),
+        in_specs=[any_space, any_space],
+        out_specs=(any_space, any_space),
+        scratch_shapes=[
+            pltpu.VMEM(rows.shape, rows.dtype),
+            pltpu.SemaphoreType.DMA((2,)),
+            pltpu.SemaphoreType.DMA((80,)),
+            pltpu.SemaphoreType.DMA((ZS * YH,)),
+            pltpu.SemaphoreType.DMA((ZS * YH,)),
+            pltpu.SemaphoreType.DMA((ZS,)),
+            pltpu.SemaphoreType.DMA((YH,)),
+        ],
+        compiler_params=pltpu.CompilerParams(collective_id=1, has_side_effects=True),
+        name="gather_row",
+    )(x, rows)
+
+
+def spread_row_kernel(x_ref, out_ref, local_sem, send_sem, recv_sem):
+    row, col = lax.axis_index("row"), lax.axis_index("col")
+    z, y = row // YH, lax.rem(row, YH)
+    tall = [(lax.rem(z + j, ZS) * YH + y, col) for j in range(1, ZS)]
+    flat = [(z * YH + lax.rem(y + j, YH), col) for j in range(1, YH)]
+    greet(tall + flat)
+    mine = pltpu.make_async_copy(x_ref, out_ref.at[z, y], local_sem)
     mine.start()
     copies = []
 
-    def send(src, slot, sem, device):
-        copy = push(src, out_ref.at[:, slot], sem, recv_sem.at[slot], device)
+    def send(src, at, where):
+        copy = push(src, out_ref.at[at], send_sem.at[len(copies)], recv_sem.at[at], where)
         copy.start()
         copies.append(copy)
 
-    def arrive(slot):
-        push(x_ref, out_ref.at[:, slot], local_sem, recv_sem.at[slot], right).wait_recv()
-
-    send(x_ref, row, z_sem.at[0, 0, 0], right)
-    send(x_ref, row, z_sem.at[1, 0, 0], left)
+    for where in tall + flat:
+        send(x_ref, (z, y), where)
+    for j in range(1, ZS):
+        there = lax.rem(z + ZS - j, ZS)
+        push(x_ref, out_ref.at[there, y], local_sem, recv_sem.at[there, y], flat[0]).wait_recv()
+        for where in flat:
+            send(out_ref.at[there, y], (there, y), where)
     for j in range(1, YH):
-        send(x_ref, row, y_sem.at[j - 1], others[j - 1])
-    for j in range(1, YH):
-        slot = z * YH + lax.rem(y + j, YH)
-        arrive(slot)
-        send(out_ref.at[:, slot], slot, z_sem.at[0, j, 0], right)
-        send(out_ref.at[:, slot], slot, z_sem.at[1, j, 0], left)
-    for hop in range(1, ZS // 2 + 1):
-        for j in range(YH):
-            lane = lax.rem(y + j, YH)
-            far_right = ZS // 2 - j % 2
-            for way, far, at, device in (
-                (0, far_right, lax.rem(z + ZS - hop, ZS), right),
-                (1, ZS - 1 - far_right, lax.rem(z + hop, ZS), left),
-            ):
-                slot = at * YH + lane
-                if hop <= far:
-                    arrive(slot)
-                if hop < far:
-                    send(out_ref.at[:, slot], slot, z_sem.at[way, j, hop], device)
+        lane = lax.rem(y + j, YH)
+        for i in range(ZS):
+            there = lax.rem(z + i, ZS)
+            push(x_ref, out_ref.at[there, lane], local_sem, recv_sem.at[there, lane], flat[0]).wait_recv()
     for copy in copies:
         copy.wait_send()
     mine.wait()
 
 
-def gather_row(x, ident):
-    supers, width_part, span = x.shape
-    return pl.pallas_call(
-        gather_row_kernel,
-        out_shape=jax.ShapeDtypeStruct((supers, ZS * YH, width_part, span), x.dtype),
+def spread_row(x, ident):
+    return pl.pallas_call(
+        spread_row_kernel,
+        out_shape=jax.ShapeDtypeStruct((ZS, YH) + x.shape, x.dtype),
         in_specs=[pl.BlockSpec(memory_space=pl.ANY)],
         out_specs=pl.BlockSpec(memory_space=pl.ANY),
         scratch_shapes=[
             pltpu.SemaphoreType.DMA,
-            pltpu.SemaphoreType.DMA((YH - 1,)),
-            pltpu.SemaphoreType.DMA((2, YH, ZS // 2)),
-            pltpu.SemaphoreType.DMA((ZS * YH,)),
+            pltpu.SemaphoreType.DMA((ZS * YH - 1,)),
+            pltpu.SemaphoreType.DMA((ZS, YH)),
         ],
         compiler_params=pltpu.CompilerParams(collective_id=ident, has_side_effects=True),
-        name="gather_row_%d" % ident,
+        name="spread_row",
     )(x)
 
 
@@ -310,7 +428,7 @@
     piece = jnp.sum(swap_row(x.reshape(YH, rows // YH, lanes), False, ident), axis=0)
     piece = piece.reshape(ZS, rows // (YH * ZS), lanes)
     piece = jnp.sum(swap_row(piece, True, ident + 1), axis=0)
-    whole = gather_row(piece[None], ident + 2).reshape(ZS, YH, -1, lanes)
+    whole = spread_row(piece, ident + 2)
     return jnp.transpose(whole, (1, 0, 2, 3)).reshape(rows, lanes)
 
 
@@ -364,7 +482,6 @@
 def per_device(inverse_block, factor_cols, occupancy, row_block, coupling, diag_inverse):
     column = lax.axis_index("col")
     core = lax.rem(column, 2)
-    row_first = (lax.axis_index("row") == 0).astype(jnp.float32)
     row_parts = lax.axis_size("row")
     col_parts = lax.axis_size("col")
     local_rows = inverse_block.shape[0]
@@ -385,10 +502,12 @@
     )
     near = jnp.transpose(near, (0, 1, 3, 2, 4)).reshape(supers, row_parts, width_part, 256)
     outgoing = lax.dynamic_slice_in_dim(near, column * tile - block_at * 128, tile, 3)
-    arrived = lax.all_to_all(outgoing, "row", split_axis=1, concat_axis=1, tiled=True)
+    outgoing = jnp.transpose(outgoing, (1, 0, 2, 3)).reshape(ZS, YH, -1, 128)
+    panel, arrived = gather_row(part, outgoing)
+    panel = panel.reshape(supers * width, span)
+    arrived = jnp.transpose(arrived.reshape(row_parts, supers, width_part, tile), (1, 0, 2, 3))
     own_rows = arrived.reshape(supers, width, tile).astype(jnp.float32)
 
-    panel = gather_row(part, 1).reshape(supers * width, span)
     term = lax.dot_general(
         inverse_block, panel, (((1,), (1,)), ((), ())), preferred_element_type=jnp.float32
     )
@@ -396,6 +515,8 @@
 
     columns = []
     chain = []
+    here = (jnp.arange(col_parts) == column) & (lax.axis_index("row") == 0)
+    here = here.astype(jnp.float32)[:, None, None]
     for s in range(supers):
         product = summed[:, s * width : (s + 1) * width]
         own = own_rows[s]
@@ -407,10 +528,8 @@
             coupled = dot_high(columns[-1], link)
             current = -(product + coupled)
             inner = dot_high(current.T, own.T) - dot_high(own, coupled)
-        embedded = lax.dynamic_update_slice(
-            jnp.zeros((width, width), jnp.float32), diag_inverse[s].T, (column * diag_cols, 0)
-        )
-        total = row_first * embedded - inner / rows_total
+        embedded = (here * diag_inverse[s].T[None]).reshape(width, width)
+        total = embedded - inner / rows_total
         if s > 0:
             total = total + dot_high(link.T, dot_high(chain[-1], link))
         columns.append(current)

time: 254 us -> 223 us (0.88)
  starting transfers between devices: 15.5 us -> 0 us
  local copies, waits for them, and re-layouts: 17 us -> 9.64 us
  Pallas kernels: 185 us -> 178 us
    all_to_all x1 -> x0, starting transfers between devices: 15.5 us -> none  [per_device(): lax.all_to_all(outgoing, 'row', split_axis=1, concat_axis=1, tiled=True)]
    pallas_call x2, Pallas kernels: 81.3 us -> 73.4 us  [the longest x1 56.7 us: gather_row(): pl.pallas_call(gather_row_kernel, out_shape=(jax.ShapeDtypeStruct((supers...]
    dynamic_update_slice x3 -> x0, local copies, waits for them, and re-layouts: 4.38 us -> none  [per_device(): lax.dynamic_update_slice(jnp.zeros((width, width), jnp.float32), diag_inv...]
    another operation x3 -> x0, local copies, waits for them, and re-layouts: 3.4 us -> none
    unnamed x8 -> x10, local copies, waits for them, and re-layouts: 3.39 us -> 0.07 us
    transpose x0 -> x5, local copies, waits for them, and re-layouts: none -> 3.06 us  [the longest x2 1.86 us: per_device(): jnp.transpose(near, (0, 1, 3, 2, 4))]
  transfers between devices with their start and end apart: 1 -> 0, of which waited for: 0 -> 0; matrix products, arithmetic and copies ran while one was open for 8% -> 0% of each run, Pallas kernels for 36% -> 0%
where the time goes in v3:
time: 223 us
  Pallas kernels  178 us (80%)
  other arithmetic  18.1 us (8%)
  matrix products  16.2 us (7%)
  local copies, waits for them, and re-layouts  9.64 us (4%)
    pallas_call x1, Pallas kernels, gather_row(): pl.pallas_call(gather_row_kernel, out_shape=(jax.ShapeDtypeStruct((supers...  56.7 us
    pallas_call x2, Pallas kernels, swap_chips(): pl.pallas_call(swap_chips_kernel, out_shape=jax.ShapeDtypeStruct(x.shape,...  52.9 us
    pallas_call x2, Pallas kernels, swap_row(): pl.pallas_call(kernel, out_shape=jax.ShapeDtypeStruct(x.shape, x.dtype),...  19.5 us
    pallas_call x1, Pallas kernels, gather_col(): pl.pallas_call(gather_col_kernel, out_shape=jax.ShapeDtypeStruct((CHIPS *...  17.8 us
    pallas_call x1, Pallas kernels, spread_row(): pl.pallas_call(spread_row_kernel, out_shape=jax.ShapeDtypeStruct((ZS, YH)...  16.7 us
    pallas_call x2, Pallas kernels, swap_core(): pl.pallas_call(swap_core_kernel, out_shape=jax.ShapeDtypeStruct(x.shape[:...  9.51 us
    dot_general x11, matrix products, dot_high(): return jnp.dot(a, b, precision=highest)  9.5 us
    add x2, other arithmetic, scatter_sum(): return jnp.sum(swap_chips(own + other, ident + 1), axis=0)  7.08 us

profile of v3, /device:TPU:6, one launch (start us, length us, event | category | flops | bytes accessed | tf_op | source)
XLA Modules:
  0.0 222.8 jit_solution(15523717454468012917)
XLA Ops:
  0.6 0.0 copy-start
  0.6 1.7 bitcast_bitcast_fusion.x_ref
  2.3 17.8 %gather_col.1.blocks_ref = bf16[16,3,10,16,128]{4,3,2,1,0:T(8,128)(2,1)} custom-call(bf16[3,10,16,128]{3,2,1,0:T(8,128)(2,1)} %bitcast_bitcast_fusion.x_ref), custom_call_target="tpu_custom_call" | custom-call | tf_op jit(solution)/shard_map/gather_col/pallas_call | solution.py:90
  20.1 4.7 %place.1 = (bf16[3,160,16,128]{3,2,1,0:T(8,128)(2,1)}, bf16[3,16,1280]{2,1,0:T(8,128)(2,1)}) custom-call(s32[3,160]{1,0:T(4,128)} %row_block_ref.1, s32[3,160]{1,0:T(4,128)} %occupancy_ref.1, s32[1]{0:T(128)} %bitcast.column_ref, bf16[16,3,10,16,128]{4,3,2,1,0:T(8,128)(2,1)} %gather_col.1.blocks_ref), custom_call_target="tpu_custom_call" | custom-call | tf_op jit(solution)/shard_map/place/pallas_call | solution.py:466
  24.8 1.2 dynamic-slice_bitcast_fusion
  26.1 0.6 copy.13
  26.7 0.5 reshape.59
  27.2 0.2 dynamic-slice_bitcast_fusion.1
  27.4 1.2 reshape.60.rows_ref
  28.6 56.7 %gather_row.1 = (bf16[3,32,16,1280]{3,2,1,0:T(8,128)(2,1)}, bf16[8,4,15,128]{3,2,1,0:T(8,128)(2,1)}) custom-call(bf16[3,16,1280]{2,1,0:T(8,128)(2,1)} %get-tuple-element.6.x_ref, bf16[8,4,15,128]{3,2,1,0:T(8,128)(2,1)} %reshape.60.rows_ref), custom_call_target="tpu_custom_call" | custom-call | tf_op jit(solution)/shard_map/gather_row/pallas_call | solution.py:220
  85.3 0.0 copy-done
  85.4 6.7 %fusion.34 = f32[1536,640]{0,1:T(8,128)} fusion(bf16[1536,1280]{1,0:T(8,128)(2,1)} %bitcast.114, bf16[640,1280]{1,0:T(8,128)(2,1)S(1)} %copy-done), kind=kOutput, calls=%fused_computation.53 | convolution fusion | flops 2516582400 | bytes 9502720 | tf_op jit(solution)/shard_map/dot_general | solution.py:511
  92.1 5.0 %swap_core_2.1 = f32[8,40,1536]{2,1,0:T(8,128)} custom-call(f32[8,2,40,1536]{3,2,1,0:T(8,128)} %bitcast.101), custom_call_target="tpu_custom_call" | custom-call | tf_op jit(solution)/shard_map/swap_core_2/pallas_call | solution.py:301
  97.1 3.7 %bitcast_add_fusion.x_ref = f32[8,40,1536]{2,1,0:T(8,128)} fusion(f32[8,40,1536]{2,1,0:T(8,128)} %swap_core_2.1, f32[8,2,40,1536]{3,2,1,0:T(8,128)} %bitcast.102, s32[]{:T(128)S(6)} %select_n.20), kind=kLoop, calls=%fused_computation.1 | loop fusion | flops 491520 | bytes 5898244 | tf_op jit(solution)/shard_map/add | solution.py:439
  100.8 29.8 %swap_chips_3.1 = f32[8,40,1536]{2,1,0:T(8,128)} custom-call(f32[8,40,1536]{2,1,0:T(8,128)} %bitcast_add_fusion.x_ref), custom_call_target="tpu_custom_call" | custom-call | tf_op jit(solution)/shard_map/swap_chips_3/pallas_call | solution.py:362
  130.6 0.0 copy-start.1
  130.6 1.8 reduce_sum.36
  132.4 0.0 copy-done.1
  132.5 0.0 copy-start.4
  132.5 0.4 fusion.15
  132.8 0.4 fusion.10
  133.2 0.7 pad_maximum_fusion.1
  133.9 0.0 copy-done.4
  134.0 0.1 mul.57
  134.0 0.1 mul.58
  134.1 1.9 bitcast_multiply_fusion
  136.1 1.5 reshape.62
  137.6 1.9 fusion
  139.5 1.0 fusion.13
  140.5 0.0 copy-start.3
  140.5 1.1 convolution_bitcast_fusion.1
  141.6 0.6 fusion.29
  142.3 0.0 copy-done.3
  142.3 0.7 fusion.3
  143.0 1.0 fusion.8
  143.9 0.0 copy-start.2
  144.0 1.3 convolution_bitcast_fusion
  145.2 0.6 fusion.26
  145.8 0.0 copy-done.2
  145.9 0.7 fusion.6
  146.5 2.0 pad_maximum_fusion
  148.5 4.5 %swap_core_4.1 = f32[8,96,512]{2,1,0:T(8,128)} custom-call(f32[8,2,96,512]{3,2,1,0:T(8,128)} %bitcast.97), custom_call_target="tpu_custom_call" | custom-call | tf_op jit(solution)/shard_map/swap_core_4/pallas_call | solution.py:301
  153.0 3.4 %bitcast_add_fusion.1.x_ref = f32[8,96,512]{2,1,0:T(8,128)} fusion(f32[8,96,512]{2,1,0:T(8,128)} %swap_core_4.1, f32[8,2,96,512]{3,2,1,0:T(8,128)} %bitcast.98, s32[]{:T(128)S(6)} %select_n.20), kind=kLoop, calls=%fused_computation.2 | loop fusion | flops 393216 | bytes 4718596 | tf_op jit(solution)/shard_map/add | solution.py:439
  156.4 23.1 %swap_chips_5.1 = f32[8,96,512]{2,1,0:T(8,128)} custom-call(f32[8,96,512]{2,1,0:T(8,128)} %bitcast_add_fusion.1.x_ref), custom_call_target="tpu_custom_call" | custom-call | tf_op jit(solution)/shard_map/swap_chips_5/pallas_call | solution.py:362
  179.5 2.2 %reduce_sum.37 = f32[96,512]{1,0:T(8,128)} reduce(f32[8,96,512]{2,1,0:T(8,128)} %swap_chips_5.1, f32[]{:T(128)} %constant.50.clone.1), dimensions={0}, to_apply=%region_1.2 | reduce | flops 344064 | bytes 1769476 | tf_op jit(solution)/shard_map/reduce_sum | solution.py:439
  181.7 10.5 %swap_row_6.1 = f32[4,24,512]{2,1,0:T(8,128)} custom-call(f32[4,24,512]{2,1,0:T(8,128)} %bitcast.110), custom_call_target="tpu_custom_call" | custom-call | tf_op jit(solution)/shard_map/swap_row_6/pallas_call | solution.py:411
  192.2 0.9 reduce_sum.38
  193.1 0.7 reshape.64.refs_0_
  193.8 9.0 %swap_row_7.1 = f32[8,3,512]{2,1,0:T(4,128)} custom-call(f32[8,3,512]{2,1,0:T(4,128)} %reshape.64.refs_0_), custom_call_target="tpu_custom_call" | custom-call | tf_op jit(solution)/shard_map/swap_row_7/pallas_call | solution.py:411
  202.8 1.5 reduce_sum.39.x_ref
  204.3 16.7 %spread_row.1 = f32[8,4,3,512]{3,2,1,0:T(4,128)} custom-call(f32[3,512]{1,0:T(4,128)} %reduce_sum.39.x_ref), custom_call_target="tpu_custom_call" | custom-call | tf_op jit(solution)/shard_map/spread_row/pallas_call | solution.py:275
  221.0 1.0 copy.17
  222.0 0.8 reshape_reshape.11
  (4 shorter events, 0.1 us)
Async XLA Ops:
  0.6 84.7 %copy-start = (bf16[640,1280]{1,0:T(8,128)(2,1)S(1)}, bf16[640,1280]{1,0:T(8,128)(2,1)}, u32[]{:S(2)}) copy-start(bf16[640,1280]{1,0:T(8,128)(2,1)} %param.6) | copy-start | bytes 4915204
  130.6 1.8 copy-start.1
  132.5 1.5 copy-start.4
  140.5 1.7 copy-start.3
  143.9 1.9 copy-start.2

commit v4 on v3

--- a/solution.py
+++ b/solution.py
@@ -7,6 +7,7 @@
 
 highest = lax.Precision.HIGHEST
 MESH = pl.DeviceIdType.MESH
+GRANT = 16 << 20
 ZS, YH = 8, 4
 CHIPS, XS = 8, 4
 
@@ -100,7 +101,7 @@
             pltpu.SemaphoreType.DMA((2, 2)),
             pltpu.SemaphoreType.DMA((CHIPS * 2,)),
         ],
-        compiler_params=pltpu.CompilerParams(collective_id=0, has_side_effects=True),
+        compiler_params=pltpu.CompilerParams(collective_id=0, has_side_effects=True, vmem_limit_bytes=GRANT),
         name="gather_col",
     )(x)
 
@@ -234,7 +235,7 @@
             pltpu.SemaphoreType.DMA((ZS,)),
             pltpu.SemaphoreType.DMA((YH,)),
         ],
-        compiler_params=pltpu.CompilerParams(collective_id=1, has_side_effects=True),
+        compiler_params=pltpu.CompilerParams(collective_id=1, has_side_effects=True, vmem_limit_bytes=GRANT),
         name="gather_row",
     )(x, rows)
 
@@ -282,34 +283,43 @@
             pltpu.SemaphoreType.DMA((ZS * YH - 1,)),
             pltpu.SemaphoreType.DMA((ZS, YH)),
         ],
-        compiler_params=pltpu.CompilerParams(collective_id=ident, has_side_effects=True),
+        compiler_params=pltpu.CompilerParams(collective_id=ident, has_side_effects=True, vmem_limit_bytes=GRANT),
         name="spread_row",
     )(x)
 
 
-def swap_core_kernel(x_ref, out_ref, send_sem, recv_sem):
+def swap_core_kernel(x_ref, out_ref, got, send_sem, recv_sem):
     row, col = lax.axis_index("row"), lax.axis_index("col")
     chip, core = col // 2, lax.rem(col, 2)
     partner = (row, chip * 2 + 1 - core)
     greet([partner])
-    copy = push(x_ref.at[:, 1 - core], out_ref, send_sem, recv_sem, partner)
+    copy = push(x_ref.at[:, 1 - core], got, send_sem, recv_sem, partner)
     copy.start()
     copy.wait()
 
+    def add(i, carry):
+        rows = pl.ds(pl.multiple_of(i * 8, 8), 8)
+        for j in range(CHIPS):
+            out_ref[j, rows] = x_ref[j, core, rows] + got[j, rows]
+        return carry
+
+    lax.fori_loop(0, x_ref.shape[2] // 8, add, 0)
+
 
 def swap_core(x, ident):
+    shape = x.shape[:1] + x.shape[2:]
     return pl.pallas_call(
         swap_core_kernel,
-        out_shape=jax.ShapeDtypeStruct(x.shape[:1] + x.shape[2:], x.dtype),
-        in_specs=[pl.BlockSpec(memory_space=pl.ANY)],
-        out_specs=pl.BlockSpec(memory_space=pl.ANY),
-        scratch_shapes=[pltpu.SemaphoreType.DMA, pltpu.SemaphoreType.DMA],
-        compiler_params=pltpu.CompilerParams(collective_id=ident, has_side_effects=True),
+        out_shape=jax.ShapeDtypeStruct(shape, x.dtype),
+        in_specs=[pl.BlockSpec(memory_space=pltpu.VMEM)],
+        out_specs=pl.BlockSpec(memory_space=pltpu.VMEM),
+        scratch_shapes=[pltpu.VMEM(shape, x.dtype), pltpu.SemaphoreType.DMA, pltpu.SemaphoreType.DMA],
+        compiler_params=pltpu.CompilerParams(collective_id=ident, has_side_effects=True, vmem_limit_bytes=GRANT),
         name="swap_core_%d" % ident,
     )(x)
 
 
-def swap_chips_kernel(x_ref, out_ref, relay, local_sem, send_sem, away_sem, turn_sem, relay_sem, half_sem, recv_sem):
+def swap_chips_kernel(x_ref, sum_ref, out_ref, relay, local_sem, send_sem, away_sem, turn_sem, relay_sem, half_sem, recv_sem):
     row, core, at = ring_position()
     chip = at(0, 0)
     rows = x_ref.shape[1]
@@ -321,8 +331,6 @@
         return (row, at(*step) * 2 + core)
 
     greet([device(step) for step in NEAR])
-    mine = pltpu.make_async_copy(x_ref.at[chip], out_ref.at[chip], local_sem)
-    mine.start()
     copies = []
 
     def send(src, dst, sem, landing, device):
@@ -351,9 +359,19 @@
         for j in range(2):
             piece = out_ref.at[at(2, dy), parts[j]]
             push(piece, piece, local_sem, half_sem.at[j, dy], device(NEAR[0])).wait_recv()
+    others = [at(*step) for step in NEAR + ((2, 0), (2, 1))]
+
+    def add(i, carry):
+        span = pl.ds(pl.multiple_of(i * 8, 8), 8)
+        total = x_ref[chip, span]
+        for other in others:
+            total = total + out_ref[other, span]
+        sum_ref[span] = total
+        return carry
+
+    lax.fori_loop(0, rows // 8, add, 0)
     for copy in copies:
         copy.wait_send()
-    mine.wait()
 
 
 def swap_chips(x, ident):
@@ -361,10 +379,11 @@
     four = pltpu.SemaphoreType.DMA((2, 2))
     return pl.pallas_call(
         swap_chips_kernel,
-        out_shape=jax.ShapeDtypeStruct(x.shape, x.dtype),
-        in_specs=[pl.BlockSpec(memory_space=pl.ANY)],
-        out_specs=pl.BlockSpec(memory_space=pl.ANY),
+        out_shape=jax.ShapeDtypeStruct(x.shape[1:], x.dtype),
+        in_specs=[pl.BlockSpec(memory_space=pltpu.VMEM)],
+        out_specs=pl.BlockSpec(memory_space=pltpu.VMEM),
         scratch_shapes=[
+            pltpu.VMEM(x.shape, x.dtype),
             pltpu.VMEM((2, 2, rows - rows // 16 * 8, lanes), x.dtype),
             pltpu.SemaphoreType.DMA,
             pltpu.SemaphoreType.DMA((len(NEAR),)),
@@ -374,12 +393,12 @@
             four,
             pltpu.SemaphoreType.DMA((chips,)),
         ],
-        compiler_params=pltpu.CompilerParams(collective_id=ident, has_side_effects=True),
+        compiler_params=pltpu.CompilerParams(collective_id=ident, has_side_effects=True, vmem_limit_bytes=GRANT),
         name="swap_chips_%d" % ident,
     )(x)
 
 
-def swap_row_kernel(along_z, x_ref, out_ref, local_sem, send_sem, recv_sem):
+def swap_row_kernel(along_z, x_ref, sum_ref, out_ref, send_sem, recv_sem):
     row, col = lax.axis_index("row"), lax.axis_index("col")
     z, y = row // YH, lax.rem(row, YH)
     count = x_ref.shape[0]
@@ -387,8 +406,6 @@
     others = [lax.rem(me + j, count) for j in range(1, count)]
     devices = [(other * YH + y if along_z else z * YH + other, col) for other in others]
     greet(devices)
-    mine = pltpu.make_async_copy(x_ref.at[me], out_ref.at[me], local_sem)
-    mine.start()
     copies = [
         push(x_ref.at[other], out_ref.at[me], send_sem.at[j], recv_sem.at[me], devices[j])
         for j, other in enumerate(others)
@@ -397,9 +414,12 @@
         copy.start()
     for j, other in enumerate(others):
         push(x_ref.at[other], out_ref.at[other], send_sem.at[j], recv_sem.at[other], devices[j]).wait_recv()
+    total = x_ref[me]
+    for other in others:
+        total = total + out_ref[other]
+    sum_ref[...] = total
     for copy in copies:
         copy.wait_send()
-    mine.wait()
 
 
 def swap_row(x, along_z, ident):
@@ -410,33 +430,30 @@
 
     return pl.pallas_call(
         kernel,
-        out_shape=jax.ShapeDtypeStruct(x.shape, x.dtype),
-        in_specs=[pl.BlockSpec(memory_space=pl.ANY)],
-        out_specs=pl.BlockSpec(memory_space=pl.ANY),
+        out_shape=jax.ShapeDtypeStruct(x.shape[1:], x.dtype),
+        in_specs=[pl.BlockSpec(memory_space=pltpu.VMEM)],
+        out_specs=pl.BlockSpec(memory_space=pltpu.VMEM),
         scratch_shapes=[
-            pltpu.SemaphoreType.DMA,
+            pltpu.VMEM(x.shape, x.dtype),
             pltpu.SemaphoreType.DMA((count - 1,)),
             pltpu.SemaphoreType.DMA((count,)),
         ],
-        compiler_params=pltpu.CompilerParams(collective_id=ident, has_side_effects=True),
+        compiler_params=pltpu.CompilerParams(collective_id=ident, has_side_effects=True, vmem_limit_bytes=GRANT),
         name="swap_row_%d" % ident,
     )(x)
 
 
 def sum_row(x, ident):
     rows, lanes = x.shape
-    piece = jnp.sum(swap_row(x.reshape(YH, rows // YH, lanes), False, ident), axis=0)
+    piece = swap_row(x.reshape(YH, rows // YH, lanes), False, ident)
     piece = piece.reshape(ZS, rows // (YH * ZS), lanes)
-    piece = jnp.sum(swap_row(piece, True, ident + 1), axis=0)
+    piece = swap_row(piece, True, ident + 1)
     whole = spread_row(piece, ident + 2)
     return jnp.transpose(whole, (1, 0, 2, 3)).reshape(rows, lanes)
 
 
-def scatter_sum(x, core, ident):
-    grid = x.reshape((CHIPS, 2) + x.shape[1:])
-    other = swap_core(grid, ident)
-    own = lax.dynamic_index_in_dim(grid, core, 1, keepdims=False)
-    return jnp.sum(swap_chips(own + other, ident + 1), axis=0)
+def scatter_sum(x, ident):
+    return swap_chips(swap_core(x.reshape((CHIPS, 2) + x.shape[1:]), ident), ident + 1)
 
 
 def place_kernel(row_block_ref, occupancy_ref, column_ref, blocks_ref, placed_ref, part_ref):
@@ -471,6 +488,7 @@
         ),
         in_specs=[smem, smem, smem, vmem],
         out_specs=(vmem, vmem),
+        compiler_params=pltpu.CompilerParams(vmem_limit_bytes=GRANT),
         name="place",
     )(row_block, occupancy, column.reshape(1).astype(jnp.int32), blocks)
 
@@ -481,7 +499,6 @@
 
 def per_device(inverse_block, factor_cols, occupancy, row_block, coupling, diag_inverse):
     column = lax.axis_index("col")
-    core = lax.rem(column, 2)
     row_parts = lax.axis_size("row")
     col_parts = lax.axis_size("col")
     local_rows = inverse_block.shape[0]
@@ -511,7 +528,7 @@
     term = lax.dot_general(
         inverse_block, panel, (((1,), (1,)), ((), ())), preferred_element_type=jnp.float32
     )
-    summed = scatter_sum(term.reshape(col_parts, tile, supers * width), core, 2)
+    summed = scatter_sum(term.reshape(col_parts, tile, supers * width), 2)
 
     columns = []
     chain = []
@@ -535,7 +552,7 @@
         columns.append(current)
         chain.append(total)
     partial = jnp.stack([t.reshape(col_parts, diag_cols, width) for t in chain], axis=1)
-    mine = scatter_sum(partial.reshape(col_parts, supers * diag_cols, width), core, 4)
+    mine = scatter_sum(partial.reshape(col_parts, supers * diag_cols, width), 4)
     diagonals = jnp.transpose(sum_row(mine, 6).reshape(supers, diag_cols, width), (0, 2, 1))
     return (jnp.stack(columns), diagonals)
 

time: 223 us -> 198 us (0.89)
  other arithmetic: 18.1 us -> 3.23 us
  Pallas kernels: 178 us -> 172 us
  matrix products: 16.2 us -> 12.1 us
    add x2 -> x0, other arithmetic: 7.08 us -> none  [scatter_sum(): return jnp.sum(swap_chips(own + other, ident + 1), axis=0)]
    reduce_sum x4 -> x0, other arithmetic: 6.4 us -> none  [the longest x2 3.99 us: scatter_sum(): return jnp.sum(swap_chips(own + other, ident + 1), axis=0)]
    dot_general x1, matrix products: 6.72 us -> 2.73 us  [per_device(): lax.dot_general(inverse_block, panel, (((1,), (1,)), ((), ())), preferred...]
    unnamed x10 -> x20, local copies, waits for them, and re-layouts: 0.07 us -> 3.34 us
where the time goes in v4:
time: 198 us; the launch traced here: 197 us
  Pallas kernels  172 us (87%)
  matrix products  12.1 us (6%)
  local copies, waits for them, and re-layouts  9.11 us (5%)
  other arithmetic  3.23 us (2%)
    pallas_call x1, Pallas kernels, gather_row(): pl.pallas_call(gather_row_kernel, out_shape=(jax.ShapeDtypeStruct((supers...  55.5 us
    pallas_call x2, Pallas kernels, swap_chips(): pl.pallas_call(swap_chips_kernel, out_shape=jax.ShapeDtypeStruct(x.shape[...  53.5 us
    pallas_call x2, Pallas kernels, swap_row(): pl.pallas_call(kernel, out_shape=jax.ShapeDtypeStruct(x.shape[1:], x.dtyp...  19.2 us
    pallas_call x1, Pallas kernels, gather_col(): pl.pallas_call(gather_col_kernel, out_shape=jax.ShapeDtypeStruct((CHIPS *...  17.1 us
    pallas_call x1, Pallas kernels, spread_row(): pl.pallas_call(spread_row_kernel, out_shape=jax.ShapeDtypeStruct((ZS, YH)...  14.6 us
    pallas_call x2, Pallas kernels, swap_core(): pl.pallas_call(swap_core_kernel, out_shape=jax.ShapeDtypeStruct(shape, x....  9.45 us
    dot_general x11, matrix products, dot_high(): return jnp.dot(a, b, precision=highest)  9.33 us

profile of v4, /device:TPU:6, one launch (start us, length us, event | category | flops | bytes accessed | tf_op | source)
XLA Modules:
  0.0 197.4 jit_solution(3241517899250489731)
XLA Ops:
  0.6 0.0 copy-start
  0.6 1.0 bitcast_bitcast_fusion.x_ref
  1.7 17.1 %gather_col.1.blocks_ref = bf16[16,3,10,16,128]{4,3,2,1,0:T(8,128)(2,1)S(1)} custom-call(bf16[3,10,16,128]{3,2,1,0:T(8,128)(2,1)S(1)} %bitcast_bitcast_fusion.x_ref), custom_call_target="tpu_custom_call" | custom-call | tf_op jit(solution)/shard_map/gather_col/pallas_call | solution.py:91
  18.8 0.0 copy-start.2
  18.8 0.7 copy-done.2
  19.5 0.0 copy-start.3
  19.5 0.7 copy-done.3
  20.2 2.6 %place.1 = (bf16[3,160,16,128]{3,2,1,0:T(8,128)(2,1)S(1)}, bf16[3,16,1280]{2,1,0:T(8,128)(2,1)S(1)}) custom-call(s32[3,160]{1,0:T(4,128)S(1)} %copy-done.2, s32[3,160]{1,0:T(4,128)S(1)} %copy-done.3, s32[1]{0:T(128)} %bitcast.column_ref, bf16[16,3,10,16,128]{4,3,2,1,0:T(8,128)(2,1)S(1)} %gather_col.1.blocks_ref), custom_call_target="tpu_custom_call" | custom-call | tf_op jit(solution)/shard_map/place/pallas_call | solution.py:483
  22.7 0.0 copy-start.1
  22.8 1.3 copy-done.1
  24.1 1.2 dynamic-slice_bitcast_fusion
  25.3 0.6 copy.13
  25.9 0.5 reshape.59
  26.5 0.2 dynamic-slice_bitcast_fusion.1
  26.6 0.5 reshape.60.rows_ref
  27.2 55.5 %gather_row.1 = (bf16[3,32,16,1280]{3,2,1,0:T(8,128)(2,1)S(1)}, bf16[8,4,15,128]{3,2,1,0:T(8,128)(2,1)S(1)}) custom-call(bf16[3,16,1280]{2,1,0:T(8,128)(2,1)S(1)} %get-tuple-element.6.x_ref, bf16[8,4,15,128]{3,2,1,0:T(8,128)(2,1)S(1)} %reshape.60.rows_ref), custom_call_target="tpu_custom_call" | custom-call | tf_op jit(solution)/shard_map/gather_row/pallas_call | solution.py:221
  82.7 0.0 copy-done
  82.7 2.7 %fusion.29 = f32[1536,640]{0,1:T(8,128)S(1)} fusion(bf16[1536,1280]{1,0:T(8,128)(2,1)S(1)} %bitcast.98, bf16[640,1280]{1,0:T(8,128)(2,1)S(1)} %copy-done), kind=kOutput, calls=%fused_computation.49 | convolution fusion | flops 2516582400 | bytes 9502720 | tf_op jit(solution)/shard_map/dot_general | solution.py:528
  85.5 0.0 copy-start.4
  85.5 5.1 %swap_core_2.1.x_ref = f32[8,40,1536]{2,1,0:T(8,128)S(1)} custom-call(f32[8,2,40,1536]{3,2,1,0:T(8,128)S(1)} %bitcast.94), custom_call_target="tpu_custom_call" | custom-call | tf_op jit(solution)/shard_map/swap_core_2/pallas_call | solution.py:311
  90.6 0.0 copy-start.9
  90.6 30.5 %swap_chips_3.1 = f32[40,1536]{1,0:T(8,128)S(1)} custom-call(f32[8,40,1536]{2,1,0:T(8,128)S(1)} %swap_core_2.1.x_ref), custom_call_target="tpu_custom_call" | custom-call | tf_op jit(solution)/shard_map/swap_chips_3/pallas_call | solution.py:380
  121.1 0.0 copy-done.4
  121.1 0.4 fusion.15
  121.5 0.4 fusion.10
  121.9 0.0 copy-start.7
  121.9 0.6 copy-done.7
  122.6 0.7 pad_maximum_fusion.1
  123.3 0.0 copy-done.9
  123.3 0.1 mul.57
  123.4 0.1 mul.58
  123.5 1.9 bitcast_multiply_fusion
  125.4 0.6 reshape.62
  126.1 1.9 fusion
  128.0 0.0 copy-start.6
  128.0 1.0 fusion.13
  129.0 1.1 convolution_bitcast_fusion.1
  130.0 0.6 fusion.26
  130.7 0.0 copy-done.6
  130.7 0.7 fusion.3
  131.4 0.0 copy-start.8
  131.4 0.0 copy-start.5
  131.4 1.0 fusion.8
  132.4 1.1 convolution_bitcast_fusion
  133.5 0.0 copy-done.8
  133.5 0.6 fusion.24
  134.1 0.0 copy-done.5
  134.1 0.7 fusion.6
  134.8 0.5 pad_maximum_fusion
  135.3 4.4 %swap_core_4.1.x_ref = f32[8,96,512]{2,1,0:T(8,128)S(1)} custom-call(f32[8,2,96,512]{3,2,1,0:T(8,128)S(1)} %bitcast.93), custom_call_target="tpu_custom_call" | custom-call | tf_op jit(solution)/shard_map/swap_core_4/pallas_call | solution.py:311
  139.7 23.0 %swap_chips_5.1 = f32[96,512]{1,0:T(8,128)S(1)} custom-call(f32[8,96,512]{2,1,0:T(8,128)S(1)} %swap_core_4.1.x_ref), custom_call_target="tpu_custom_call" | custom-call | tf_op jit(solution)/shard_map/swap_chips_5/pallas_call | solution.py:380
  162.7 10.1 %swap_row_6.1 = f32[24,512]{1,0:T(8,128)S(1)} custom-call(f32[4,24,512]{2,1,0:T(8,128)S(1)} %bitcast.96), custom_call_target="tpu_custom_call" | custom-call | tf_op jit(solution)/shard_map/swap_row_6/pallas_call | solution.py:431
  172.8 9.1 %swap_row_7.1.x_ref = f32[3,512]{1,0:T(4,128)S(1)} custom-call(f32[8,3,512]{2,1,0:T(4,128)S(1)} %reshape.64.refs_0_), custom_call_target="tpu_custom_call" | custom-call | tf_op jit(solution)/shard_map/swap_row_7/pallas_call | solution.py:431
  181.9 14.6 %spread_row.1 = f32[8,4,3,512]{3,2,1,0:T(4,128)S(1)} custom-call(f32[3,512]{1,0:T(4,128)S(1)} %swap_row_7.1.x_ref), custom_call_target="tpu_custom_call" | custom-call | tf_op jit(solution)/shard_map/spread_row/pallas_call | solution.py:276
  196.6 0.8 reshape_reshape.11
  (6 shorter events, 0.2 us)
Async XLA Ops:
  0.6 82.1 %copy-start = (bf16[640,1280]{1,0:T(8,128)(2,1)S(1)}, bf16[640,1280]{1,0:T(8,128)(2,1)}, u32[]{:S(2)}) copy-start(bf16[640,1280]{1,0:T(8,128)(2,1)} %param.6) | copy-start | bytes 4915204
  18.8 0.7 copy-start.2
  19.5 0.7 copy-start.3
  22.7 1.3 copy-start.1
  85.5 35.7 %copy-start.4 = (bf16[2,512,512]{2,1,0:T(8,128)(2,1)S(1)}, bf16[2,512,512]{2,1,0:T(8,128)(2,1)}, u32[]{:S(2)}) copy-start(bf16[2,512,512]{2,1,0:T(8,128)(2,1)} %param.10) | copy-start | bytes 3145732
  90.6 32.7 %copy-start.9 = (f32[3,512,32]{1,2,0:T(8,128)S(1)}, f32[3,512,32]{1,2,0:T(8,128)}, u32[]{:S(2)}) copy-start(f32[3,512,32]{1,2,0:T(8,128)} %param.11) | copy-start | bytes 589828
  121.9 0.6 copy-start.7
  128.0 2.7 %copy-start.6 = (f32[512,512]{1,0:T(8,128)S(1)}, f32[512,512]{1,0:T(8,128)}, u32[]{:S(2)}) copy-start(f32[512,512]{1,0:T(8,128)} %get-tuple-element.20) | copy-start | bytes 3145732
  131.4 2.1 %copy-start.8 = (f32[40,512]{1,0:T(8,128)S(1)}, f32[40,512]{1,0:T(8,128)}, u32[]{:S(2)}) copy-start(f32[40,512]{1,0:T(8,128)} %copy-done.7) | copy-start | bytes 245764
  131.4 2.7 %copy-start.5 = (f32[512,512]{1,0:T(8,128)S(1)}, f32[512,512]{1,0:T(8,128)}, u32[]{:S(2)}) copy-start(f32[512,512]{1,0:T(8,128)} %get-tuple-element.19) | copy-start | bytes 3145732

commit v5 on v4

--- a/solution.py
+++ b/solution.py
@@ -106,7 +106,7 @@
     )(x)
 
 
-def gather_row_kernel(x_ref, rows_ref, out_ref, own_ref, staged, local_sem, send_sem, wide_sem, thin_sem, z_sem, y_sem):
+def gather_row_kernel(x_ref, out_ref, local_sem, send_sem, wide_sem, thin_sem):
     row, col = lax.axis_index("row"), lax.axis_index("col")
     z, y = row // YH, lax.rem(row, YH)
     last = x_ref.shape[0] - 1
@@ -119,12 +119,10 @@
     def device(dz, dy):
         return (at(dz, dy), col)
 
-    zs, ys = range(1, ZS), range(1, YH)
-    greet([device(dz, 0) for dz in zs] + [device(0, dy) for dy in ys])
-    locals_ = [pltpu.make_async_copy(x_ref, out_ref.at[:, row], local_sem.at[0])]
-    locals_.append(pltpu.make_async_copy(rows_ref.at[z], staged.at[z], local_sem.at[1]))
-    for copy in locals_:
-        copy.start()
+    right, left, up, down = device(1, 0), device(-1, 0), device(0, 1), device(0, -1)
+    greet([right, left, up, down])
+    mine = pltpu.make_async_copy(x_ref, out_ref.at[:, row], local_sem)
+    mine.start()
     copies = []
 
     def send(src, dst, landing, where):
@@ -141,9 +139,8 @@
 
     def arrive(kind, slot):
         piece = block(kind, slot)
-        push(piece, piece, local_sem.at[0], sems[kind].at[slot], device(1, 0)).wait_recv()
-
-    right, left, up, down = device(1, 0), device(-1, 0), device(0, 1), device(0, -1)
+        push(piece, piece, local_sem, sems[kind].at[slot], right).wait_recv()
+
     for where in (right, left):
         onward(1, row, where, True)
     for where in (up, down):
@@ -152,9 +149,6 @@
         onward(0, row, where, True)
     for where in (up, down):
         onward(1, row, where, True)
-    for dz in zs:
-        there = lax.rem(z + dz, ZS)
-        send(rows_ref.at[there], staged.at[z], z_sem.at[z], device(dz, 0))
 
     for dy in (-1, 1, 2):
         slot = at(0, dy)
@@ -193,98 +187,29 @@
         cross(hop - 1)
         if hop > 1:
             cross(1 - hop)
-        if hop == 1:
-            locals_[1].wait()
-            for dz in zs:
-                there = lax.rem(z + dz, ZS)
-                push(rows_ref.at[there], staged.at[there], local_sem.at[1], z_sem.at[there], right).wait_recv()
-            keep = pltpu.make_async_copy(staged.at[:, y], own_ref.at[:, y], local_sem.at[1])
-            keep.start()
-            for dy in ys:
-                there = lax.rem(y + dy, YH)
-                send(staged.at[:, there], own_ref.at[:, y], y_sem.at[y], device(0, dy))
     cross(half)
     for dz in range(1 - half, half + 1):
         arrive(1, at(dz, 2))
-    for dy in ys:
-        there = lax.rem(y + dy, YH)
-        push(staged.at[:, there], own_ref.at[:, there], local_sem.at[1], y_sem.at[there], right).wait_recv()
-    for copy in copies:
-        copy.wait_send()
-    locals_[0].wait()
-    keep.wait()
-
-
-def gather_row(x, rows):
-    supers, width_part, span = x.shape
-    any_space = pl.BlockSpec(memory_space=pl.ANY)
-    return pl.pallas_call(
-        gather_row_kernel,
-        out_shape=(
-            jax.ShapeDtypeStruct((supers, ZS * YH, width_part, span), x.dtype),
-            jax.ShapeDtypeStruct(rows.shape, rows.dtype),
-        ),
-        in_specs=[any_space, any_space],
-        out_specs=(any_space, any_space),
-        scratch_shapes=[
-            pltpu.VMEM(rows.shape, rows.dtype),
-            pltpu.SemaphoreType.DMA((2,)),
-            pltpu.SemaphoreType.DMA((80,)),
-            pltpu.SemaphoreType.DMA((ZS * YH,)),
-            pltpu.SemaphoreType.DMA((ZS * YH,)),
-            pltpu.SemaphoreType.DMA((ZS,)),
-            pltpu.SemaphoreType.DMA((YH,)),
-        ],
-        compiler_params=pltpu.CompilerParams(collective_id=1, has_side_effects=True, vmem_limit_bytes=GRANT),
-        name="gather_row",
-    )(x, rows)
-
-
-def spread_row_kernel(x_ref, out_ref, local_sem, send_sem, recv_sem):
-    row, col = lax.axis_index("row"), lax.axis_index("col")
-    z, y = row // YH, lax.rem(row, YH)
-    tall = [(lax.rem(z + j, ZS) * YH + y, col) for j in range(1, ZS)]
-    flat = [(z * YH + lax.rem(y + j, YH), col) for j in range(1, YH)]
-    greet(tall + flat)
-    mine = pltpu.make_async_copy(x_ref, out_ref.at[z, y], local_sem)
-    mine.start()
-    copies = []
-
-    def send(src, at, where):
-        copy = push(src, out_ref.at[at], send_sem.at[len(copies)], recv_sem.at[at], where)
-        copy.start()
-        copies.append(copy)
-
-    for where in tall + flat:
-        send(x_ref, (z, y), where)
-    for j in range(1, ZS):
-        there = lax.rem(z + ZS - j, ZS)
-        push(x_ref, out_ref.at[there, y], local_sem, recv_sem.at[there, y], flat[0]).wait_recv()
-        for where in flat:
-            send(out_ref.at[there, y], (there, y), where)
-    for j in range(1, YH):
-        lane = lax.rem(y + j, YH)
-        for i in range(ZS):
-            there = lax.rem(z + i, ZS)
-            push(x_ref, out_ref.at[there, lane], local_sem, recv_sem.at[there, lane], flat[0]).wait_recv()
     for copy in copies:
         copy.wait_send()
     mine.wait()
 
 
-def spread_row(x, ident):
+def gather_row(x):
+    supers, width_part, span = x.shape
     return pl.pallas_call(
-        spread_row_kernel,
-        out_shape=jax.ShapeDtypeStruct((ZS, YH) + x.shape, x.dtype),
+        gather_row_kernel,
+        out_shape=jax.ShapeDtypeStruct((supers, ZS * YH, width_part, span), x.dtype),
         in_specs=[pl.BlockSpec(memory_space=pl.ANY)],
         out_specs=pl.BlockSpec(memory_space=pl.ANY),
         scratch_shapes=[
             pltpu.SemaphoreType.DMA,
-            pltpu.SemaphoreType.DMA((ZS * YH - 1,)),
-            pltpu.SemaphoreType.DMA((ZS, YH)),
+            pltpu.SemaphoreType.DMA((80,)),
+            pltpu.SemaphoreType.DMA((ZS * YH,)),
+            pltpu.SemaphoreType.DMA((ZS * YH,)),
         ],
-        compiler_params=pltpu.CompilerParams(collective_id=ident, has_side_effects=True, vmem_limit_bytes=GRANT),
-        name="spread_row",
+        compiler_params=pltpu.CompilerParams(collective_id=1, has_side_effects=True, vmem_limit_bytes=GRANT),
+        name="gather_row",
     )(x)
 
 
@@ -319,7 +244,47 @@
     )(x)
 
 
-def swap_chips_kernel(x_ref, sum_ref, out_ref, relay, local_sem, send_sem, away_sem, turn_sem, relay_sem, half_sem, recv_sem):
+class RowExchange:
+    def __init__(self, rows_ref, own_ref, staged, local_sem, send_sem, z_sem, y_sem):
+        self.rows, self.own, self.staged = rows_ref, own_ref, staged
+        self.local_sem, self.send_sem, self.z_sem, self.y_sem = local_sem, send_sem, z_sem, y_sem
+        row, self.col = lax.axis_index("row"), lax.axis_index("col")
+        self.z, self.y = row // YH, lax.rem(row, YH)
+        self.over_z = [lax.rem(self.z + j, ZS) for j in range(1, ZS)]
+        self.over_y = [lax.rem(self.y + j, YH) for j in range(1, YH)]
+        self.z_devices = [(other * YH + self.y, self.col) for other in self.over_z]
+        self.y_devices = [(self.z * YH + other, self.col) for other in self.over_y]
+        self.copies = []
+
+    def send(self, *args):
+        copy = push(*args)
+        copy.start()
+        self.copies.append(copy)
+
+    def begin(self):
+        self.mine = pltpu.make_async_copy(self.rows.at[self.z], self.staged.at[self.z], self.local_sem)
+        self.mine.start()
+        for j, other in enumerate(self.over_z):
+            self.send(self.rows.at[other], self.staged.at[self.z], self.send_sem.at[j], self.z_sem.at[self.z], self.z_devices[j])
+
+    def turn(self):
+        self.mine.wait()
+        for j, other in enumerate(self.over_z):
+            push(self.rows.at[other], self.staged.at[other], self.local_sem, self.z_sem.at[other], self.z_devices[j]).wait_recv()
+        self.mine = pltpu.make_async_copy(self.staged.at[:, self.y], self.own.at[:, self.y], self.local_sem)
+        self.mine.start()
+        for j, other in enumerate(self.over_y):
+            self.send(self.staged.at[:, other], self.own.at[:, self.y], self.send_sem.at[ZS - 1 + j], self.y_sem.at[self.y], self.y_devices[j])
+
+    def end(self):
+        for j, other in enumerate(self.over_y):
+            push(self.staged.at[:, other], self.own.at[:, other], self.local_sem, self.y_sem.at[other], self.y_devices[j]).wait_recv()
+        for copy in self.copies:
+            copy.wait_send()
+        self.mine.wait()
+
+
+def swap_chips_kernel(x_ref, sum_ref, out_ref, relay, local_sem, send_sem, away_sem, turn_sem, relay_sem, half_sem, recv_sem, ride=None):
     row, core, at = ring_position()
     chip = at(0, 0)
     rows = x_ref.shape[1]
@@ -330,7 +295,9 @@
     def device(step):
         return (row, at(*step) * 2 + core)
 
-    greet([device(step) for step in NEAR])
+    greet([device(step) for step in NEAR] + (ride.z_devices + ride.y_devices if ride else []))
+    if ride:
+        ride.begin()
     copies = []
 
     def send(src, dst, sem, landing, device):
@@ -352,6 +319,8 @@
             push(held(j, dy), held(j, dy), local_sem, relay_sem.at[j, dy], device(NEAR[j])).wait_recv()
             target = device((NEAR[j][0], dy))
             send(held(j, dy), out_ref.at[origin, parts[j]], turn_sem.at[j, dy], half_sem.at[j, dy], target)
+    if ride:
+        ride.turn()
     for step in NEAR:
         other = at(*step)
         push(x_ref.at[other], out_ref.at[other], local_sem, recv_sem.at[other], device(step)).wait_recv()
@@ -372,91 +341,134 @@
     lax.fori_loop(0, rows // 8, add, 0)
     for copy in copies:
         copy.wait_send()
-
-
-def swap_chips(x, ident):
-    chips, rows, lanes = x.shape
-    four = pltpu.SemaphoreType.DMA((2, 2))
+    if ride:
+        ride.end()
+
+
+def swap_chips(x, ident, rows=None):
+    chips, tall, lanes = x.shape
+    dma = pltpu.SemaphoreType.DMA
+    shapes = [jax.ShapeDtypeStruct(x.shape[1:], x.dtype)]
+    scratch = [
+        pltpu.VMEM(x.shape, x.dtype),
+        pltpu.VMEM((2, 2, tall - tall // 16 * 8, lanes), x.dtype),
+        dma,
+        dma((len(NEAR),)),
+        dma((2, 2)),
+        dma((2, 2)),
+        dma((2, 2)),
+        dma((2, 2)),
+        dma((chips,)),
+    ]
+    own = len(scratch)
+    operands = [x]
+    if rows is not None:
+        operands.append(rows)
+        shapes.append(jax.ShapeDtypeStruct(rows.shape, rows.dtype))
+        scratch += [pltpu.VMEM(rows.shape, rows.dtype), dma, dma((ZS + YH - 2,)), dma((ZS,)), dma((YH,))]
+
+    def kernel(*refs):
+        count = len(operands)
+        arrays, rest = refs[: 2 * count], refs[2 * count :]
+        ride = RowExchange(arrays[1], arrays[3], *rest[own:]) if count == 2 else None
+        swap_chips_kernel(arrays[0], arrays[count], *rest[:own], ride=ride)
+
+    vmem = pl.BlockSpec(memory_space=pltpu.VMEM)
     return pl.pallas_call(
-        swap_chips_kernel,
-        out_shape=jax.ShapeDtypeStruct(x.shape[1:], x.dtype),
-        in_specs=[pl.BlockSpec(memory_space=pltpu.VMEM)],
-        out_specs=pl.BlockSpec(memory_space=pltpu.VMEM),
+        kernel,
+        out_shape=shapes,
+        in_specs=[vmem] * len(operands),
+        out_specs=[vmem] * len(operands),
+        scratch_shapes=scratch,
+        compiler_params=pltpu.CompilerParams(collective_id=ident, has_side_effects=True, vmem_limit_bytes=GRANT),
+        name="swap_chips_%d" % ident,
+    )(*operands)
+
+
+def sum_row_kernel(x_ref, out_ref, got_y, mid, got_z, whole, y_send, y_recv, z_send, z_recv, send_sem, recv_sem):
+    row, col = lax.axis_index("row"), lax.axis_index("col")
+    z, y = row // YH, lax.rem(row, YH)
+    zs = [lax.rem(z + j, ZS) for j in range(1, ZS)]
+    ys = [lax.rem(y + j, YH) for j in range(1, YH)]
+    tall = [(other * YH + y, col) for other in zs]
+    flat = [(z * YH + other, col) for other in ys]
+    greet(tall + flat)
+    copies = []
+
+    def send(*args):
+        copy = push(*args)
+        copy.start()
+        copies.append(copy)
+
+    for j, other in enumerate(ys):
+        send(x_ref.at[other], got_y.at[y], y_send.at[j], y_recv.at[y], flat[j])
+    for j, other in enumerate(ys):
+        push(x_ref.at[other], got_y.at[other], y_send.at[j], y_recv.at[other], flat[j]).wait_recv()
+    total = x_ref[y]
+    for other in ys:
+        total = total + got_y[other]
+    mid[...] = total
+    for j, other in enumerate(zs):
+        send(mid.at[other], got_z.at[z], z_send.at[j], z_recv.at[z], tall[j])
+    for j, other in enumerate(zs):
+        push(mid.at[other], got_z.at[other], z_send.at[j], z_recv.at[other], tall[j]).wait_recv()
+    total = mid[z]
+    for other in zs:
+        total = total + got_z[other]
+    whole[...] = total
+    out_ref[z, y] = total
+    first = len(copies)
+
+    def spread(src, at, where):
+        send(src, out_ref.at[at], send_sem.at[len(copies) - first], recv_sem.at[at], where)
+
+    for where in tall + flat:
+        spread(whole, (z, y), where)
+    for j in range(1, ZS):
+        there = lax.rem(z + ZS - j, ZS)
+        push(whole, out_ref.at[there, y], y_send.at[0], recv_sem.at[there, y], flat[0]).wait_recv()
+        for where in flat:
+            spread(out_ref.at[there, y], (there, y), where)
+    for lane in ys:
+        for there in [z] + zs:
+            push(whole, out_ref.at[there, lane], y_send.at[0], recv_sem.at[there, lane], flat[0]).wait_recv()
+    for copy in copies:
+        copy.wait_send()
+
+
+def sum_row(x, ident):
+    rows, lanes = x.shape
+    grid = x.reshape(YH, ZS, rows // (YH * ZS), lanes)
+    dma = pltpu.SemaphoreType.DMA
+    vmem = pl.BlockSpec(memory_space=pltpu.VMEM)
+    whole = pl.pallas_call(
+        sum_row_kernel,
+        out_shape=jax.ShapeDtypeStruct((ZS, YH) + grid.shape[2:], x.dtype),
+        in_specs=[vmem],
+        out_specs=vmem,
         scratch_shapes=[
-            pltpu.VMEM(x.shape, x.dtype),
-            pltpu.VMEM((2, 2, rows - rows // 16 * 8, lanes), x.dtype),
-            pltpu.SemaphoreType.DMA,
-            pltpu.SemaphoreType.DMA((len(NEAR),)),
-            four,
-            four,
-            four,
-            four,
-            pltpu.SemaphoreType.DMA((chips,)),
+            pltpu.VMEM(grid.shape, x.dtype),
+            pltpu.VMEM(grid.shape[1:], x.dtype),
+            pltpu.VMEM(grid.shape[1:], x.dtype),
+            pltpu.VMEM(grid.shape[2:], x.dtype),
+            dma((YH - 1,)),
+            dma((YH,)),
+            dma((ZS - 1,)),
+            dma((ZS,)),
+            dma((ZS * YH - 1,)),
+            dma((ZS, YH)),
         ],
         compiler_params=pltpu.CompilerParams(collective_id=ident, has_side_effects=True, vmem_limit_bytes=GRANT),
-        name="swap_chips_%d" % ident,
-    )(x)
-
-
-def swap_row_kernel(along_z, x_ref, sum_ref, out_ref, send_sem, recv_sem):
-    row, col = lax.axis_index("row"), lax.axis_index("col")
-    z, y = row // YH, lax.rem(row, YH)
-    count = x_ref.shape[0]
-    me = z if along_z else y
-    others = [lax.rem(me + j, count) for j in range(1, count)]
-    devices = [(other * YH + y if along_z else z * YH + other, col) for other in others]
-    greet(devices)
-    copies = [
-        push(x_ref.at[other], out_ref.at[me], send_sem.at[j], recv_sem.at[me], devices[j])
-        for j, other in enumerate(others)
-    ]
-    for copy in copies:
-        copy.start()
-    for j, other in enumerate(others):
-        push(x_ref.at[other], out_ref.at[other], send_sem.at[j], recv_sem.at[other], devices[j]).wait_recv()
-    total = x_ref[me]
-    for other in others:
-        total = total + out_ref[other]
-    sum_ref[...] = total
-    for copy in copies:
-        copy.wait_send()
-
-
-def swap_row(x, along_z, ident):
-    count = x.shape[0]
-
-    def kernel(*refs):
-        swap_row_kernel(along_z, *refs)
-
-    return pl.pallas_call(
-        kernel,
-        out_shape=jax.ShapeDtypeStruct(x.shape[1:], x.dtype),
-        in_specs=[pl.BlockSpec(memory_space=pltpu.VMEM)],
-        out_specs=pl.BlockSpec(memory_space=pltpu.VMEM),
-        scratch_shapes=[
-            pltpu.VMEM(x.shape, x.dtype),
-            pltpu.SemaphoreType.DMA((count - 1,)),
-            pltpu.SemaphoreType.DMA((count,)),
-        ],
-        compiler_params=pltpu.CompilerParams(collective_id=ident, has_side_effects=True, vmem_limit_bytes=GRANT),
-        name="swap_row_%d" % ident,
-    )(x)
-
-
-def sum_row(x, ident):
-    rows, lanes = x.shape
-    piece = swap_row(x.reshape(YH, rows // YH, lanes), False, ident)
-    piece = piece.reshape(ZS, rows // (YH * ZS), lanes)
-    piece = swap_row(piece, True, ident + 1)
-    whole = spread_row(piece, ident + 2)
+        name="sum_row",
+    )(grid)
     return jnp.transpose(whole, (1, 0, 2, 3)).reshape(rows, lanes)
 
 
-def scatter_sum(x, ident):
-    return swap_chips(swap_core(x.reshape((CHIPS, 2) + x.shape[1:]), ident), ident + 1)
-
-
-def place_kernel(row_block_ref, occupancy_ref, column_ref, blocks_ref, placed_ref, part_ref):
+def scatter_sum(x, ident, rows=None):
+    return swap_chips(swap_core(x.reshape((CHIPS, 2) + x.shape[1:]), ident), ident + 1, rows)
+
+
+def place_kernel(row_block_ref, occupancy_ref, start_ref, blocks_ref, near_ref, part_ref, placed_ref):
     supers, nblocks = placed_ref.shape[:2]
     per = blocks_ref.shape[2]
     for s in range(supers):
@@ -470,27 +482,36 @@
             return carry
 
         lax.fori_loop(0, nblocks // per, step, 0)
-    first = column_ref[0] * per
+    first, block_at = start_ref[0], start_ref[1]
+    row_parts = near_ref.shape[1]
     for s in range(supers):
+
+        def around(r, carry, s=s):
+            for k in range(2):
+                near_ref[s, r, :, k * 128 : (k + 1) * 128] = placed_ref[s, r * (nblocks // row_parts) + block_at + k]
+            return carry
+
+        lax.fori_loop(0, row_parts, around, 0)
         for k in range(per):
             part_ref[s, :, k * 128 : (k + 1) * 128] = placed_ref[s, first + k]
 
 
-def place(blocks, occupancy, row_block, column):
+def place(blocks, occupancy, row_block, starts, row_parts):
     devices, supers, per, width_part, tall = blocks.shape
     smem = pl.BlockSpec(memory_space=pltpu.SMEM)
     vmem = pl.BlockSpec(memory_space=pltpu.VMEM)
     return pl.pallas_call(
         place_kernel,
         out_shape=(
-            jax.ShapeDtypeStruct((supers, devices * per, width_part, tall), blocks.dtype),
+            jax.ShapeDtypeStruct((supers, row_parts, width_part, 2 * tall), blocks.dtype),
             jax.ShapeDtypeStruct((supers, width_part, per * tall), blocks.dtype),
         ),
         in_specs=[smem, smem, smem, vmem],
         out_specs=(vmem, vmem),
+        scratch_shapes=[pltpu.VMEM((supers, devices * per, width_part, tall), blocks.dtype)],
         compiler_params=pltpu.CompilerParams(vmem_limit_bytes=GRANT),
         name="place",
-    )(row_block, occupancy, column.reshape(1).astype(jnp.int32), blocks)
+    )(row_block, occupancy, starts, blocks)
 
 
 def dot_high(a, b):
@@ -510,25 +531,18 @@
     per = span // 128
 
     packed = jnp.transpose(factor_cols.reshape(supers, per, 128, width_part), (0, 1, 3, 2))
-    placed, part = place(gather_col(packed), occupancy, row_block, column)
-
-    per_row = local_rows // 128
-    block_at = jnp.minimum(column * tile // 128, per_row - 2)
-    near = lax.dynamic_slice_in_dim(
-        placed.reshape(supers, row_parts, per_row, width_part, 128), block_at, 2, 2
-    )
-    near = jnp.transpose(near, (0, 1, 3, 2, 4)).reshape(supers, row_parts, width_part, 256)
+    block_at = jnp.minimum(column * tile // 128, local_rows // 128 - 2)
+    starts = jnp.stack([column * per, block_at]).astype(jnp.int32)
+    near, part = place(gather_col(packed), occupancy, row_block, starts, row_parts)
     outgoing = lax.dynamic_slice_in_dim(near, column * tile - block_at * 128, tile, 3)
     outgoing = jnp.transpose(outgoing, (1, 0, 2, 3)).reshape(ZS, YH, -1, 128)
-    panel, arrived = gather_row(part, outgoing)
-    panel = panel.reshape(supers * width, span)
-    arrived = jnp.transpose(arrived.reshape(row_parts, supers, width_part, tile), (1, 0, 2, 3))
-    own_rows = arrived.reshape(supers, width, tile).astype(jnp.float32)
-
+    panel = gather_row(part).reshape(supers * width, span)
     term = lax.dot_general(
         inverse_block, panel, (((1,), (1,)), ((), ())), preferred_element_type=jnp.float32
     )
-    summed = scatter_sum(term.reshape(col_parts, tile, supers * width), 2)
+    summed, arrived = scatter_sum(term.reshape(col_parts, tile, supers * width), 2, outgoing)
+    arrived = jnp.transpose(arrived.reshape(row_parts, supers, width_part, tile), (1, 0, 2, 3))
+    own_rows = arrived.reshape(supers, width, tile).astype(jnp.float32)
 
     columns = []
     chain = []
@@ -552,7 +566,7 @@
         columns.append(current)
         chain.append(total)
     partial = jnp.stack([t.reshape(col_parts, diag_cols, width) for t in chain], axis=1)
-    mine = scatter_sum(partial.reshape(col_parts, supers * diag_cols, width), 4)
+    (mine,) = scatter_sum(partial.reshape(col_parts, supers * diag_cols, width), 4)
     diagonals = jnp.transpose(sum_row(mine, 6).reshape(supers, diag_cols, width), (0, 2, 1))
     return (jnp.stack(columns), diagonals)
 

time: 198 us -> 197 us (level)
  Pallas kernels: 172 us -> 169 us
    pallas_call x7 -> x5, Pallas kernels: 145 us -> 142 us  [the longest x2 55.5 us: swap_chips(): pl.pallas_call(kernel, out_shape=shapes, in_specs=[vmem] * len(operands),...]
    unnamed x20 -> x16, local copies, waits for them, and re-layouts: 3.34 us -> 4.22 us
where the time goes in v5:
time: 197 us; the launch traced here: 196 us
  Pallas kernels  169 us (86%)
  matrix products  12.9 us (7%)
  local copies, waits for them, and re-layouts  10.9 us (6%)
  other arithmetic  2.31 us (1%)
    pallas_call x2, Pallas kernels, swap_chips(): pl.pallas_call(kernel, out_shape=shapes, in_specs=[vmem] * len(operands),...  55.5 us
    pallas_call x1, Pallas kernels, gather_row(): pl.pallas_call(gather_row_kernel, out_shape=jax.ShapeDtypeStruct((supers,...  53.9 us
    pallas_call x1, Pallas kernels, sum_row(): pl.pallas_call(sum_row_kernel, out_shape=jax.ShapeDtypeStruct((ZS, YH) +...  30 us
    pallas_call x1, Pallas kernels, gather_col(): pl.pallas_call(gather_col_kernel, out_shape=jax.ShapeDtypeStruct((CHIPS *...  17.1 us
    dot_general x11, matrix products, dot_high(): return jnp.dot(a, b, precision=highest)  10.2 us
    pallas_call x2, Pallas kernels, swap_core(): pl.pallas_call(swap_core_kernel, out_shape=jax.ShapeDtypeStruct(shape, x....  9.32 us
    unnamed x16, local copies, waits for them, and re-layouts  4.22 us

profile of v5, /device:TPU:6, one launch (start us, length us, event | category | flops | bytes accessed | tf_op | source)
XLA Modules:
  0.0 196.0 jit_solution(16301002243234582481)
XLA Ops:
  0.6 0.0 copy-start
  0.7 0.1 pad_add_fusion.start_ref
  0.7 1.0 bitcast_bitcast_fusion.x_ref
  1.8 17.1 %gather_col.1.blocks_ref = bf16[16,3,10,16,128]{4,3,2,1,0:T(8,128)(2,1)S(1)} custom-call(bf16[3,10,16,128]{3,2,1,0:T(8,128)(2,1)S(1)} %bitcast_bitcast_fusion.x_ref), custom_call_target="tpu_custom_call" | custom-call | tf_op jit(solution)/shard_map/gather_col/pallas_call | solution.py:91
  18.9 0.0 copy-start.3
  18.9 0.7 copy-done.3
  19.6 0.0 copy-start.4
  19.6 0.7 copy-done.4
  20.2 3.2 %place.1 = (bf16[3,32,16,256]{3,2,1,0:T(8,128)(2,1)S(1)}, bf16[3,16,1280]{2,1,0:T(8,128)(2,1)S(1)}) custom-call(s32[3,160]{1,0:T(4,128)S(1)} %copy-done.3, s32[3,160]{1,0:T(4,128)S(1)} %copy-done.4, s32[2]{0:T(128)S(1)} %pad_add_fusion.start_ref, bf16[16,3,10,16,128]{4,3,2,1,0:T(8,128)(2,1)S(1)} %gather_col.1.blocks_ref), custom_call_target="tpu_custom_call" | custom-call | tf_op jit(solution)/shard_map/place/pallas_call | solution.py:503
  23.4 53.9 %gather_row.1 = bf16[3,32,16,1280]{3,2,1,0:T(8,128)(2,1)S(1)} custom-call(bf16[3,16,1280]{2,1,0:T(8,128)(2,1)S(1)} %get-tuple-element.6.x_ref), custom_call_target="tpu_custom_call" | custom-call | tf_op jit(solution)/shard_map/gather_row/pallas_call | solution.py:200
  77.3 0.0 copy-done
  77.3 2.7 %fusion.29 = f32[1536,640]{0,1:T(8,128)S(1)} fusion(bf16[1536,1280]{1,0:T(8,128)(2,1)S(1)} %bitcast.89, bf16[640,1280]{1,0:T(8,128)(2,1)S(1)} %copy-done), kind=kOutput, calls=%fused_computation.49 | convolution fusion | flops 2516582400 | bytes 9502720 | tf_op jit(solution)/shard_map/dot_general | solution.py:540
  80.1 5.0 %swap_core_2.1.refs_0_ = f32[8,40,1536]{2,1,0:T(8,128)S(1)} custom-call(f32[8,2,40,1536]{3,2,1,0:T(8,128)S(1)} %bitcast.90), custom_call_target="tpu_custom_call" | custom-call | tf_op jit(solution)/shard_map/swap_core_2/pallas_call | solution.py:236
  85.0 0.0 copy-start.1
  85.1 1.3 copy-done.1
  86.3 0.0 copy-start.5
  86.3 0.2 dynamic-slice_bitcast_fusion
  86.6 0.5 reshape.46.refs_1_
  87.1 0.0 copy-start.2
  87.1 1.5 copy-done.2
  88.6 32.5 %swap_chips_3.1 = (f32[40,1536]{1,0:T(8,128)S(1)}, bf16[8,4,15,128]{3,2,1,0:T(8,128)(2,1)S(1)}) custom-call(f32[8,40,1536]{2,1,0:T(8,128)S(1)} %copy-done.2, bf16[8,4,15,128]{3,2,1,0:T(8,128)(2,1)S(1)} %reshape.46.refs_1_), custom_call_target="tpu_custom_call" | custom-call | tf_op jit(solution)/shard_map/swap_chips_3/pallas_call | solution.py:377
  121.1 1.4 reshape.47
  122.5 1.1 fusion.28
  123.5 0.0 copy-done.5
  123.5 0.4 fusion.15
  123.9 0.4 fusion.10
  124.3 1.6 fusion.24
  125.9 1.6 fusion.26
  127.5 0.1 mul.61
  127.6 0.7 mul.62
  128.3 0.9 slice_bitcast_fusion
  129.2 1.0 bitcast_multiply_fusion
  130.1 0.7 fusion
  130.8 0.0 copy-start.7
  130.9 1.0 fusion.13
  131.8 1.1 convolution_bitcast_fusion.1
  132.9 0.0 copy-done.7
  132.9 0.7 fusion.3
  133.7 0.0 copy-start.6
  133.7 1.0 fusion.8
  134.7 1.1 convolution_bitcast_fusion
  135.8 0.0 copy-done.6
  135.8 0.7 fusion.6
  136.5 0.5 pad_maximum_fusion
  137.0 4.4 %swap_core_4.1.refs_0_ = f32[8,96,512]{2,1,0:T(8,128)S(1)} custom-call(f32[8,2,96,512]{3,2,1,0:T(8,128)S(1)} %bitcast.88), custom_call_target="tpu_custom_call" | custom-call | tf_op jit(solution)/shard_map/swap_core_4/pallas_call | solution.py:236
  141.4 23.0 %swap_chips_5.1 = f32[96,512]{1,0:T(8,128)S(1)} custom-call(f32[8,96,512]{2,1,0:T(8,128)S(1)} %swap_core_4.1.refs_0_), custom_call_target="tpu_custom_call" | custom-call | tf_op jit(solution)/shard_map/swap_chips_5/pallas_call | solution.py:377
  164.4 0.1 reshape.48.x_ref
  164.5 30.0 %sum_row.1 = f32[8,4,3,512]{3,2,1,0:T(4,128)S(1)} custom-call(f32[4,8,3,512]{3,2,1,0:T(4,128)S(1)} %reshape.48.x_ref), custom_call_target="tpu_custom_call" | custom-call | tf_op jit(solution)/shard_map/sum_row/pallas_call | solution.py:444
  194.5 0.8 reshape_reshape.11
  195.3 0.7 pad_maximum_fusion.1
  (4 shorter events, 0.1 us)
Async XLA Ops:
  0.6 76.7 %copy-start = (bf16[640,1280]{1,0:T(8,128)(2,1)S(1)}, bf16[640,1280]{1,0:T(8,128)(2,1)}, u32[]{:S(2)}) copy-start(bf16[640,1280]{1,0:T(8,128)(2,1)} %param.6) | copy-start | bytes 4915204
  18.9 0.7 copy-start.3
  19.6 0.7 copy-start.4
  85.0 1.3 copy-start.1
  86.3 37.2 %copy-start.5 = (bf16[2,512,512]{2,1,0:T(8,128)(2,1)S(1)}, bf16[2,512,512]{2,1,0:T(8,128)(2,1)}, u32[]{:S(2)}) copy-start(bf16[2,512,512]{2,1,0:T(8,128)(2,1)} %param.10) | copy-start | bytes 3145732
  87.1 1.5 copy-start.2
  130.8 2.1 %copy-start.7 = (f32[512,512]{1,0:T(8,128)S(1)}, f32[512,512]{1,0:T(8,128)}, u32[]{:S(2)}) copy-start(f32[512,512]{1,0:T(8,128)} %fusion.26) | copy-start | bytes 3145732
  133.7 2.1 %copy-start.6 = (f32[512,512]{1,0:T(8,128)S(1)}, f32[512,512]{1,0:T(8,128)}, u32[]{:S(2)}) copy-start(f32[512,512]{1,0:T(8,128)} %fusion.24) | copy-start | bytes 3145732

commit v6 on v5

--- a/solution.py
+++ b/solution.py
@@ -400,21 +400,21 @@
         copy.start()
         copies.append(copy)
 
+    for j, other in enumerate(zs):
+        send(x_ref.at[other], got_z.at[z], z_send.at[j], z_recv.at[z], tall[j])
+    for j, other in enumerate(zs):
+        push(x_ref.at[other], got_z.at[other], z_send.at[j], z_recv.at[other], tall[j]).wait_recv()
+    total = x_ref[z]
+    for other in zs:
+        total = total + got_z[other]
+    mid[...] = total
     for j, other in enumerate(ys):
-        send(x_ref.at[other], got_y.at[y], y_send.at[j], y_recv.at[y], flat[j])
+        send(mid.at[other], got_y.at[y], y_send.at[j], y_recv.at[y], flat[j])
     for j, other in enumerate(ys):
-        push(x_ref.at[other], got_y.at[other], y_send.at[j], y_recv.at[other], flat[j]).wait_recv()
-    total = x_ref[y]
+        push(mid.at[other], got_y.at[other], y_send.at[j], y_recv.at[other], flat[j]).wait_recv()
+    total = mid[y]
     for other in ys:
         total = total + got_y[other]
-    mid[...] = total
-    for j, other in enumerate(zs):
-        send(mid.at[other], got_z.at[z], z_send.at[j], z_recv.at[z], tall[j])
-    for j, other in enumerate(zs):
-        push(mid.at[other], got_z.at[other], z_send.at[j], z_recv.at[other], tall[j]).wait_recv()
-    total = mid[z]
-    for other in zs:
-        total = total + got_z[other]
     whole[...] = total
     out_ref[z, y] = total
     first = len(copies)
@@ -422,15 +422,14 @@
     def spread(src, at, where):
         send(src, out_ref.at[at], send_sem.at[len(copies) - first], recv_sem.at[at], where)
 
-    for where in tall + flat:
+    for where in flat + tall:
         spread(whole, (z, y), where)
-    for j in range(1, ZS):
-        there = lax.rem(z + ZS - j, ZS)
-        push(whole, out_ref.at[there, y], y_send.at[0], recv_sem.at[there, y], flat[0]).wait_recv()
-        for where in flat:
-            spread(out_ref.at[there, y], (there, y), where)
     for lane in ys:
-        for there in [z] + zs:
+        push(whole, out_ref.at[z, lane], y_send.at[0], recv_sem.at[z, lane], flat[0]).wait_recv()
+        for where in tall:
+            spread(out_ref.at[z, lane], (z, lane), where)
+    for there in zs:
+        for lane in [y] + ys:
             push(whole, out_ref.at[there, lane], y_send.at[0], recv_sem.at[there, lane], flat[0]).wait_recv()
     for copy in copies:
         copy.wait_send()
@@ -438,7 +437,7 @@
 
 def sum_row(x, ident):
     rows, lanes = x.shape
-    grid = x.reshape(YH, ZS, rows // (YH * ZS), lanes)
+    grid = x.reshape(ZS, YH, rows // (YH * ZS), lanes)
     dma = pltpu.SemaphoreType.DMA
     vmem = pl.BlockSpec(memory_space=pltpu.VMEM)
     whole = pl.pallas_call(
@@ -447,9 +446,9 @@
         in_specs=[vmem],
         out_specs=vmem,
         scratch_shapes=[
-            pltpu.VMEM(grid.shape, x.dtype),
             pltpu.VMEM(grid.shape[1:], x.dtype),
             pltpu.VMEM(grid.shape[1:], x.dtype),
+            pltpu.VMEM(grid.shape, x.dtype),
             pltpu.VMEM(grid.shape[2:], x.dtype),
             dma((YH - 1,)),
             dma((YH,)),
@@ -461,7 +460,7 @@
         compiler_params=pltpu.CompilerParams(collective_id=ident, has_side_effects=True, vmem_limit_bytes=GRANT),
         name="sum_row",
     )(grid)
-    return jnp.transpose(whole, (1, 0, 2, 3)).reshape(rows, lanes)
+    return whole.reshape(rows, lanes)
 
 
 def scatter_sum(x, ident, rows=None):

time: 197 us -> 196 us (level)
  Pallas kernels: 169 us -> 167 us
    unnamed x16 -> x20, local copies, waits for them, and re-layouts: 4.22 us -> 4.24 us
where the time goes in v6:
time: 196 us; the launch traced here: 195 us
  Pallas kernels  167 us (85%)
  matrix products  12.9 us (7%)
  local copies, waits for them, and re-layouts  10.9 us (6%)
  other arithmetic  2.31 us (1%)
    pallas_call x2, Pallas kernels, swap_chips(): pl.pallas_call(kernel, out_shape=shapes, in_specs=[vmem] * len(operands),...  55.5 us
    pallas_call x1, Pallas kernels, gather_row(): pl.pallas_call(gather_row_kernel, out_shape=jax.ShapeDtypeStruct((supers,...  53.9 us
    pallas_call x1, Pallas kernels, sum_row(): pl.pallas_call(sum_row_kernel, out_shape=jax.ShapeDtypeStruct((ZS, YH) +...  28.4 us
    pallas_call x1, Pallas kernels, gather_col(): pl.pallas_call(gather_col_kernel, out_shape=jax.ShapeDtypeStruct((CHIPS *...  17.1 us
    dot_general x11, matrix products, dot_high(): return jnp.dot(a, b, precision=highest)  10.2 us
    pallas_call x2, Pallas kernels, swap_core(): pl.pallas_call(swap_core_kernel, out_shape=jax.ShapeDtypeStruct(shape, x....  9.45 us
    unnamed x20, local copies, waits for them, and re-layouts  4.24 us

profile of v6, /device:TPU:6, one launch (start us, length us, event | category | flops | bytes accessed | tf_op | source)
XLA Modules:
  0.0 194.6 jit_solution(2612510663990874313)
XLA Ops:
  0.6 0.0 copy-start
  0.7 0.1 pad_add_fusion.start_ref
  0.7 1.0 bitcast_bitcast_fusion.x_ref
  1.8 17.1 %gather_col.1.blocks_ref = bf16[16,3,10,16,128]{4,3,2,1,0:T(8,128)(2,1)S(1)} custom-call(bf16[3,10,16,128]{3,2,1,0:T(8,128)(2,1)S(1)} %bitcast_bitcast_fusion.x_ref), custom_call_target="tpu_custom_call" | custom-call | tf_op jit(solution)/shard_map/gather_col/pallas_call | solution.py:91
  18.9 0.0 copy-start.3
  18.9 0.7 copy-done.3
  19.6 0.0 copy-start.4
  19.6 0.7 copy-done.4
  20.2 3.2 %place.1 = (bf16[3,32,16,256]{3,2,1,0:T(8,128)(2,1)S(1)}, bf16[3,16,1280]{2,1,0:T(8,128)(2,1)S(1)}) custom-call(s32[3,160]{1,0:T(4,128)S(1)} %copy-done.3, s32[3,160]{1,0:T(4,128)S(1)} %copy-done.4, s32[2]{0:T(128)S(1)} %pad_add_fusion.start_ref, bf16[16,3,10,16,128]{4,3,2,1,0:T(8,128)(2,1)S(1)} %gather_col.1.blocks_ref), custom_call_target="tpu_custom_call" | custom-call | tf_op jit(solution)/shard_map/place/pallas_call | solution.py:502
  23.4 53.9 %gather_row.1 = bf16[3,32,16,1280]{3,2,1,0:T(8,128)(2,1)S(1)} custom-call(bf16[3,16,1280]{2,1,0:T(8,128)(2,1)S(1)} %get-tuple-element.6.x_ref), custom_call_target="tpu_custom_call" | custom-call | tf_op jit(solution)/shard_map/gather_row/pallas_call | solution.py:200
  77.3 0.0 copy-done
  77.3 2.7 %fusion.29 = f32[1536,640]{0,1:T(8,128)S(1)} fusion(bf16[1536,1280]{1,0:T(8,128)(2,1)S(1)} %bitcast.88, bf16[640,1280]{1,0:T(8,128)(2,1)S(1)} %copy-done), kind=kOutput, calls=%fused_computation.49 | convolution fusion | flops 2516582400 | bytes 9502720 | tf_op jit(solution)/shard_map/dot_general | solution.py:539
  80.1 5.0 %swap_core_2.1.refs_0_ = f32[8,40,1536]{2,1,0:T(8,128)S(1)} custom-call(f32[8,2,40,1536]{3,2,1,0:T(8,128)S(1)} %bitcast.89), custom_call_target="tpu_custom_call" | custom-call | tf_op jit(solution)/shard_map/swap_core_2/pallas_call | solution.py:236
  85.0 0.0 copy-start.1
  85.1 1.3 copy-done.1
  86.4 0.0 copy-start.5
  86.4 0.2 dynamic-slice_bitcast_fusion
  86.6 0.5 reshape.46.refs_1_
  87.1 0.0 copy-start.2
  87.1 1.5 copy-done.2
  88.7 32.5 %swap_chips_3.1 = (f32[40,1536]{1,0:T(8,128)S(1)}, bf16[8,4,15,128]{3,2,1,0:T(8,128)(2,1)S(1)}) custom-call(f32[8,40,1536]{2,1,0:T(8,128)S(1)} %copy-done.2, bf16[8,4,15,128]{3,2,1,0:T(8,128)(2,1)S(1)} %reshape.46.refs_1_), custom_call_target="tpu_custom_call" | custom-call | tf_op jit(solution)/shard_map/swap_chips_3/pallas_call | solution.py:377
  121.1 1.4 reshape.47
  122.5 1.1 fusion.28
  123.6 0.0 copy-done.5
  123.6 0.4 fusion.15
  123.9 0.4 fusion.10
  124.3 0.0 copy-start.8
  124.3 1.6 fusion.24
  125.9 1.6 fusion.26
  127.6 0.1 mul.61
  127.6 0.7 mul.62
  128.3 0.9 slice_bitcast_fusion
  129.2 1.0 bitcast_multiply_fusion
  130.2 0.7 fusion
  130.9 0.0 copy-start.7
  130.9 1.0 fusion.13
  131.9 1.1 convolution_bitcast_fusion.1
  133.0 0.0 copy-done.7
  133.0 0.7 fusion.3
  133.7 0.0 copy-start.6
  133.7 1.0 fusion.8
  134.7 1.1 convolution_bitcast_fusion
  135.8 0.0 copy-done.8
  135.8 0.0 copy-done.6
  135.8 0.7 fusion.6
  136.5 0.5 pad_maximum_fusion
  137.1 0.0 copy-start.9
  137.1 4.5 %swap_core_4.1.refs_0_ = f32[8,96,512]{2,1,0:T(8,128)S(1)} custom-call(f32[8,2,96,512]{3,2,1,0:T(8,128)S(1)} %bitcast.87), custom_call_target="tpu_custom_call" | custom-call | tf_op jit(solution)/shard_map/swap_core_4/pallas_call | solution.py:236
  141.6 23.0 %swap_chips_5.1 = f32[96,512]{1,0:T(8,128)S(1)} custom-call(f32[8,96,512]{2,1,0:T(8,128)S(1)} %swap_core_4.1.refs_0_), custom_call_target="tpu_custom_call" | custom-call | tf_op jit(solution)/shard_map/swap_chips_5/pallas_call | solution.py:377
  164.6 0.1 reshape.48.x_ref
  164.7 28.4 %sum_row.1 = f32[8,4,3,512]{3,2,1,0:T(4,128)S(1)} custom-call(f32[8,4,3,512]{3,2,1,0:T(4,128)S(1)} %reshape.48.x_ref), custom_call_target="tpu_custom_call" | custom-call | tf_op jit(solution)/shard_map/sum_row/pallas_call | solution.py:443
  193.0 0.8 reshape_reshape.11
  193.8 0.0 copy-done.9
  193.9 0.7 pad_maximum_fusion.1
  (3 shorter events, 0.1 us)
Async XLA Ops:
  0.6 76.7 %copy-start = (bf16[640,1280]{1,0:T(8,128)(2,1)S(1)}, bf16[640,1280]{1,0:T(8,128)(2,1)}, u32[]{:S(2)}) copy-start(bf16[640,1280]{1,0:T(8,128)(2,1)} %param.6) | copy-start | bytes 4915204
  18.9 0.7 copy-start.3
  19.6 0.7 copy-start.4
  85.0 1.3 copy-start.1
  86.4 37.2 %copy-start.5 = (bf16[2,512,512]{2,1,0:T(8,128)(2,1)S(1)}, bf16[2,512,512]{2,1,0:T(8,128)(2,1)}, u32[]{:S(2)}) copy-start(bf16[2,512,512]{2,1,0:T(8,128)(2,1)} %param.10) | copy-start | bytes 3145732
  87.1 1.5 copy-start.2
  124.3 11.5 %copy-start.8 = (f32[40,512]{1,0:T(8,128)}, f32[40,512]{1,0:T(8,128)S(1)}, u32[]{:S(2)}) copy-start(f32[40,512]{1,0:T(8,128)S(1)} %fusion.10) | copy-start | bytes 245764
  130.9 2.1 %copy-start.7 = (f32[512,512]{1,0:T(8,128)S(1)}, f32[512,512]{1,0:T(8,128)}, u32[]{:S(2)}) copy-start(f32[512,512]{1,0:T(8,128)} %fusion.26) | copy-start | bytes 3145732
  133.7 2.1 %copy-start.6 = (f32[512,512]{1,0:T(8,128)S(1)}, f32[512,512]{1,0:T(8,128)}, u32[]{:S(2)}) copy-start(f32[512,512]{1,0:T(8,128)} %fusion.24) | copy-start | bytes 3145732
  137.1 56.8 %copy-start.9 = (f32[40,512]{1,0:T(8,128)S(1)}, f32[40,512]{1,0:T(8,128)}, u32[]{:S(2)}) copy-start(f32[40,512]{1,0:T(8,128)} %copy-done.8) | copy-start | bytes 245764
